TPU v7x, 32 devices: a whole 2x2x4 slice. The times are simulated.
32 devices in a mesh: stream: 4 (over y, core), azim: 8 (over z, x).
Axes of the slice: x: 2, y: 2, z: 4, core: 2. Of those that a mesh axis runs over, the one named last changes fastest.
Arguments:
- fluid: float32 [4, 256, 256, 128], P(None, 'stream', 'azim'), may hold values from -4 to 4
- bubbles: float32 [16384, 5, 128], P(('stream', 'azim'))
- counts: int32 [32], P(('stream', 'azim')), may hold values from 128 to 512
- outgoing_block_order: int32 [16384], P(('stream', 'azim')), may hold values from 0 to 511, as said below
- tiles_first_update: int32 [16384], P(('stream', 'azim')), may hold values from 0 to 2047
- tiles_after: int32 [16384], P(('stream', 'azim')), may hold values from 0 to 2047
Outputs:
- fluid_out: float32 [4, 256, 256, 128], P(None, 'stream', 'azim')
- bubbles_out: float32 [16384, 5, 128], P(('stream', 'azim'))
- void_fraction: float32 [256, 256, 128], P('stream', 'azim')
Inputs may be any that keep to these rules, and one draw needn't show every extreme that they name: `outgoing_block_order`: for each device, its 512 entries are each of 0 to 511 once.
All inputs are finite; a program needn't handle non-finite values.
Results may differ from a plain program's by a relative error of at most 0.000076.
Values sent between devices are 32-bit elements; how exact they have to be, the bound alone decides.
A program may use at most 128 MiB of HBM per device.

v0:
```python
import functools

import jax
import jax.numpy as jnp
from jax import lax
from jax.experimental import pallas as pl
from jax.experimental.pallas import tpu as pltpu
from jax.sharding import PartitionSpec as P

MESH = pl.DeviceIdType.MESH
SUBSTEPS = 8
TIME_STEP = 0.25
MEAN_FLOW = 0.5
DIFFUSION = 0.1
KERNEL_WIDTH = 1.5
GAS_INDEX = 4.2
PRESSURE_COUPLING = 0.3
AMBIENT = 1.0
RELAX_TIME = 0.5
VISCOUS = 0.08
SOURCE_GAIN = 0.05
VOID_SCALE = 0.01
FOUR_PI = 12.566370614359172
LOG2E = 1.4426950408889634
SHARPNESS = 0.5 * LOG2E / (KERNEL_WIDTH * KERNEL_WIDTH)
GROUP = 8
QUAD = 4
CHUNK = 16
STATES = 5
WIDE = 4
VMEM_GRANT = 60 * 2**20
f32, bf16 = jnp.float32, jnp.bfloat16


def cell_columns(cells_n, lanes):
    column = lax.broadcasted_iota(jnp.int32, (8, lanes), 0).astype(f32)
    tiles = cells_n // 8
    return {a: column + float(8 * a) for a in centres(tiles)}


def centres(tiles):
    return [min(start + 1, tiles - 1) for start in range(0, tiles, 3)]


def raw_weights(position, columns, tiles):
    pieces = [None] * tiles
    for start in range(0, tiles, 3):
        width = min(3, tiles - start)
        middle = min(start + 1, tiles - 1)
        offset = columns[middle] - position
        slope = offset * -SHARPNESS
        at = slope * offset
        pieces[middle] = jnp.exp2(at)
        if width > 1:
            near = at - 64.0 * SHARPNESS
            step = slope * 16.0
            pieces[middle - 1] = jnp.exp2(near - step)
            if middle + 1 < start + width:
                pieces[middle + 1] = jnp.exp2(near + step)
    return jnp.concatenate(pieces, axis=0)


def split_bf16(values):
    high = values.astype(bf16)
    low = (values - high.astype(f32)).astype(bf16)
    return high, low


def two_parts(rows):
    high = rows.astype(bf16).astype(f32)
    return jnp.concatenate([high, rows - high], axis=0).astype(bf16)


def clear_lhs(lhs):
    cells_n = lhs.shape[2] // 2
    lhs[...] = jnp.zeros_like(lhs)
    one = jnp.ones((1, cells_n), f32)
    for q in range(lhs.shape[0]):
        lhs[q, 4:5, :cells_n] = one
        lhs[q, 12:13, cells_n:] = one


def sample_quad(q, at, positions, columns, rows_of, lhs, sp, su, sn):
    cells_n = lhs.shape[2] // 2
    weights = []
    for j in range(QUAD):
        p_row, u_row = rows_of(j)
        row, side = 8 * (j // 2) + 2 * (j % 2), slice(cells_n * (j // 2), cells_n * (j // 2 + 1))
        lhs[q, row : row + 1, side] = p_row
        lhs[q, row + 1 : row + 2, side] = u_row
        weights.append(raw_weights(positions[j], columns, cells_n // 8).astype(bf16))
    rhs = jnp.concatenate(
        [jnp.concatenate(weights[:2], axis=1), jnp.concatenate(weights[2:], axis=1)], axis=0
    )
    result = jnp.dot(two_parts(lhs[q]), rhs, preferred_element_type=f32)
    result = result[:16] + result[16:]
    lanes = rhs.shape[1] // 2
    for j in range(QUAD):
        row, part = 8 * (j // 2), result[:, lanes * (j % 2) : lanes * (j % 2 + 1)]
        first = row + 2 * (j % 2)
        sp[pl.ds(at + j, 1), :] = part[first : first + 1]
        su[pl.ds(at + j, 1), :] = part[first + 1 : first + 2]
        sn[pl.ds(at + j, 1), :] = part[row + 4 : row + 5]


def advance_group(state, pressure, velocity, norm):
    radius, growth, position, speed, rest = state
    inverse = 1.0 / norm
    drive = AMBIENT + PRESSURE_COUPLING * (pressure * inverse)
    velocity = velocity * inverse
    h = TIME_STEP / SUBSTEPS
    for _ in range(SUBSTEPS):
        over = 1.0 / radius
        gas = jnp.exp(GAS_INDEX * jnp.log(rest * over))
        accel = (gas - drive - 1.5 * growth * growth - VISCOUS * growth * over) * over
        growth = growth + h * accel
        radius = radius + h * growth
        speed = speed + (h / RELAX_TIME) * (velocity - speed)
        position = position + h * speed
    return radius, growth, position, speed, rest


def source_amount(radius, growth):
    return SOURCE_GAIN * FOUR_PI * radius * radius * growth


def void_amount(radius):
    return VOID_SCALE * FOUR_PI / 3.0 * radius * radius * radius


def spread_pair(pair, positions, amounts, columns, tiles):
    pieces, norms = [], []
    for position in positions:
        raw = raw_weights(position, columns, tiles)
        norms.append(jnp.sum(raw, axis=0, keepdims=True))
        pieces.append(jnp.concatenate(split_bf16(raw), axis=1))
    rhs = jnp.concatenate(pieces, axis=0)
    sublane = lax.broadcasted_iota(jnp.int32, amounts[0].shape, 0)
    inverse = 1.0 / jnp.where(sublane == 2 * pair, norms[0], norms[1])
    rows = jnp.concatenate([a * inverse for a in amounts], axis=0)
    lhs = two_parts(rows)
    lhs = jnp.concatenate([lhs, lhs], axis=1)
    result = lax.dot_general(
        lhs, rhs, (((1,), (1,)), ((), ())), preferred_element_type=f32
    )
    result = result[: rows.shape[0]] + result[rows.shape[0] :]
    cells_n = 8 * tiles
    out = []
    for n in range(len(amounts)):
        for side in range(2):
            row = GROUP * n + 2 * pair + side
            out.append(result[row : row + 1, side * cells_n : (side + 1) * cells_n])
    return out


def lanes_of(rows):
    number, lanes = rows.shape
    pieces = []
    for at in range(0, number, lanes):
        block = rows[at : at + lanes]
        same = lax.broadcasted_iota(jnp.int32, block.shape, 0) == lax.broadcasted_iota(
            jnp.int32, block.shape, 1
        )
        line = jnp.sum(jnp.where(same, block, 0.0), axis=0, keepdims=True)
        pieces.append(line[:, : block.shape[0]])
    return jnp.concatenate(pieces, axis=1)


def scatter(tile_rows, parts, outs):
    tiles = outs[0].shape[0]
    cells_n = outs[0].shape[1]
    ids = lanes_of(tile_rows[...])
    block = min(256, tiles)
    rhs = jnp.concatenate([x for part in parts for x in split_bf16(part[...])], axis=1)

    def some(i, carry):
        at = pl.multiple_of(i * block, block)
        tile = lax.broadcasted_iota(jnp.int32, (block, ids.shape[1]), 0) + at
        hot = jnp.where(tile.astype(f32) == ids, 1.0, 0.0).astype(bf16)
        result = jnp.dot(hot, rhs, preferred_element_type=f32)
        for n, out in enumerate(outs):
            high = result[:, 2 * n * cells_n : (2 * n + 1) * cells_n]
            out[pl.ds(at, block), :] = high + result[:, (2 * n + 1) * cells_n : (2 * n + 2) * cells_n]
        return carry

    lax.fori_loop(0, tiles // block, some, 0)


def flow_plane(s, width, fluid, left, right, source, store):
    comps, _, cells = fluid.shape
    row = lax.broadcasted_iota(jnp.int32, (width, cells), 0)
    lane = lax.broadcasted_iota(jnp.int32, (width, cells), 1)

    def plane(ref, c, n):
        return ref[c, pl.ds(pl.multiple_of(n * width, width), width), :]

    d_s, d_a, d_r, lap, now = [], [], [], [], []
    for c in range(comps):
        x, below, above = (plane(fluid, c, s + n) for n in (1, 0, 2))
        a_down = jnp.where(row == 0, left[c, pl.ds(s, 1), :], pltpu.roll(x, 1, 0))
        a_up = jnp.where(row == width - 1, right[c, pl.ds(s, 1), :], pltpu.roll(x, width - 1, 0))
        r_down = jnp.where(lane == 0, 0.0, pltpu.roll(x, 1, 1))
        r_up = jnp.where(lane == cells - 1, 0.0, pltpu.roll(x, cells - 1, 1))
        now.append(x)
        d_s.append(above - below)
        d_a.append(a_up - a_down)
        d_r.append(r_up - r_down)
        lap.append(above + below + a_up + a_down + r_up + r_down - 6.0 * x)
    half = 0.5 * TIME_STEP
    change = [
        MEAN_FLOW * d_s[0] + d_s[1] + d_a[2] + d_r[3],
        MEAN_FLOW * d_s[1] + d_s[0],
        MEAN_FLOW * d_s[2] + d_a[0],
        MEAN_FLOW * d_s[3] + d_r[0],
    ]
    for c in range(comps):
        new = now[c] - half * change[c] + DIFFUSION * lap[c]
        if c == 0:
            new = new - TIME_STEP * source[pl.ds(pl.multiple_of(s * width, width), width), :]
        store(c, new)


def peer_of(n, streams, azims):
    turn, other = n // streams, n % streams
    step = (turn + 1) // 2 * (2 * (turn % 2) - 1)
    away = (azims // 2 + step + azims) % azims
    stream = (lax.axis_index("stream") + (other + 1) % streams) % streams
    return stream, (lax.axis_index("azim") + away) % azims


def first_kernel(streams, azims, cap, length, width,
                 order_ref, tiles_ref, count_ref, bubbles_hbm, fluid_hbm,
                 fluid_out, arrived, low_out, high_out, left_out, right_out,
                 fluid_v, new_v, low_v, high_v, left_v, right_v, first_v, last_v, zero_v,
                 bubbles_v, now_v, live_v, tile_v, amount_v, place_v, sp, su, sn, send_v, spread_v,
                 source_v, lhs, load_sems, store_sem, own_sem, zero_sems, send_sems, recv_sems,
                 early_send, early_recv, late_send, late_recv):
    devices = streams * azims
    comps, cells_n = fluid_hbm.shape[0], fluid_hbm.shape[2]
    slots, lanes = sp.shape
    stream, azim = lax.axis_index("stream"), lax.axis_index("azim")
    me = stream * azims + azim
    last_stream = streams - 1

    barrier = pltpu.get_barrier_semaphore()

    def greet(n, carry):
        other = (me + n) % devices
        pl.semaphore_signal(
            barrier, inc=1, device_id=(other // azims, other % azims), device_id_type=MESH
        )
        return carry

    lax.fori_loop(1, devices, greet, 0)
    inner = pl.ds(width, length * width)
    loads = [
        pltpu.make_async_copy(fluid_hbm, fluid_v.at[:, inner], load_sems.at[0]),
        pltpu.make_async_copy(bubbles_hbm, bubbles_v, load_sems.at[1]),
    ]
    for load in loads:
        load.start()
    clear_lhs(lhs)
    zero_v[...] = jnp.zeros_like(zero_v)

    @pl.when(stream == 0)
    def _():
        low_v[...] = jnp.zeros_like(low_v)

    @pl.when(stream == last_stream)
    def _():
        high_v[...] = jnp.zeros_like(high_v)

    columns = cell_columns(cells_n, lanes)
    tiles = cells_n // 8
    per = max(1, CHUNK // cap)
    chunk = per * cap
    chunks = slots // chunk
    for load in loads:
        load.wait()

    def sample(i):
        for q in range(chunk // QUAD):
            positions = []

            def rows_of(j, q=q):
                k = q * QUAD + j
                peer_stream, peer_azim = peer_of(i * per + k // cap, streams, azims)
                slot = (peer_stream * azims + peer_azim) * cap + k % cap
                block = order_ref[slot]
                tile = tiles_ref[block]
                at = i * chunk + k
                for c in range(STATES):
                    now_v[c, pl.ds(at, 1), :] = bubbles_v[pl.ds(c * slots + block, 1), :]
                live = jnp.where(block < count_ref[0], 1.0, 0.0)
                live_v[pl.ds(at, 1), :] = jnp.full((1, lanes), live, f32)
                tile_v[pl.ds(at, 1), :] = jnp.full((1, lanes), tile.astype(f32), f32)
                row = tile + width
                positions.append(bubbles_v[pl.ds(2 * slots + block, 1), :])
                return fluid_v[0, pl.ds(row, 1), :], fluid_v[comps - 1, pl.ds(row, 1), :]

            rows = [rows_of(j) for j in range(QUAD)]
            at = i * chunk + q * QUAD
            sample_quad(q, at, positions, columns, lambda j: rows[j], lhs, sp, su, sn)

    def advance(i):
        for g in range(chunk // GROUP):
            at = pl.ds(pl.multiple_of(i * chunk + g * GROUP, GROUP), GROUP)
            live = live_v[at, :] > 0.5
            state = [now_v[c, at, :] for c in range(STATES)]
            state[0] = jnp.where(live, state[0], 1.0)
            state[4] = jnp.where(live, state[4], 1.0)
            new = advance_group(state, sp[at, :], su[at, :], sn[at, :])
            amount_v[at, :] = jnp.where(live, source_amount(new[0], new[1]), 0.0)
            place_v[at, :] = new[2]
            new = (jnp.where(live, new[0], -1.0),) + tuple(new[1:])
            piece = min(cap, GROUP)
            for k in range(0, GROUP, piece):
                n = g * GROUP + k
                for c in range(STATES):
                    send_v[i * per + n // cap, c, n % cap : n % cap + piece, :] = new[c][k : k + piece]

    def spread(i):
        for g in range(chunk // GROUP):
            base = pl.multiple_of(i * chunk + g * GROUP, GROUP)
            amount = amount_v[pl.ds(base, GROUP), :]
            for pair in range(GROUP // 2):
                positions = [place_v[pl.ds(base + 2 * pair + n, 1), :] for n in range(2)]
                rows = spread_pair(pair, positions, [amount], columns, tiles)
                for n in range(2):
                    spread_v[pl.ds(base + 2 * pair + n, 1), :] = rows[n]

    def to_peer(n):
        peer = peer_of(n, streams, azims)
        return pltpu.make_async_remote_copy(
            src_ref=send_v.at[n], dst_ref=arrived.at[me], send_sem=send_sems.at[n],
            recv_sem=recv_sems.at[me], device_id=peer, device_id_type=MESH,
        )

    def from_peer(other):
        return pltpu.make_async_remote_copy(
            src_ref=send_v.at[0], dst_ref=arrived.at[other], send_sem=send_sems.at[0],
            recv_sem=recv_sems.at[other], device_id=(other // azims, other % azims),
            device_id_type=MESH,
        )

    own = pltpu.make_async_copy(send_v.at[devices - 1], arrived.at[me], own_sem)

    def send(i, end=False):
        for q in range(per):
            if end and q == per - 1:
                own.start()
            else:
                to_peer(i * per + q).start()

    def halo_copies(ends, cols, lands, sends, recvs):
        def copy(n, src, dst, peer):
            return pltpu.make_async_remote_copy(
                src_ref=src, dst_ref=dst, send_sem=sends.at[n], recv_sem=recvs.at[n],
                device_id=peer, device_id_type=MESH,
            )

        up, down = (stream + 1) % streams, (stream + streams - 1) % streams
        right, left = (azim + 1) % azims, (azim + azims - 1) % azims
        return (
            copy(0, ends[1], lands[0], (up, azim)),
            copy(1, ends[0], lands[1], (down, azim)),
            copy(2, cols[1], lands[2], (stream, right)),
            copy(3, cols[0], lands[3], (stream, left)),
        )

    def halo_start(copies):
        pl.when(stream < last_stream)(copies[0].start)
        pl.when(stream > 0)(copies[1].start)
        copies[2].start()
        copies[3].start()

    def halo_sent(copies):
        pl.when(stream < last_stream)(copies[0].wait_send)
        pl.when(stream > 0)(copies[1].wait_send)
        copies[2].wait_send()
        copies[3].wait_send()

    def halo_here(copies):
        pl.when(stream > 0)(copies[0].wait_recv)
        pl.when(stream < last_stream)(copies[1].wait_recv)
        copies[2].wait_recv()
        copies[3].wait_recv()

    def ends_of(ref, first):
        return [ref.at[:, pl.ds(width * n, width)] for n in (first, first + length - 1)]

    sample(0)
    def edge(s, carry):
        at = pl.multiple_of((s + 1) * width, width)
        for c in range(comps):
            first_v[c, pl.ds(s, 1), :] = fluid_v[c, pl.ds(at, 1), :]
            last_v[c, pl.ds(s, 1), :] = fluid_v[c, pl.ds(at + width - 1, 1), :]
        return carry

    lax.fori_loop(0, length, edge, 0)
    sample(1)
    advance(0)
    pl.semaphore_wait(barrier, devices - 1)
    early = halo_copies(ends_of(fluid_v, 1), (first_v, last_v), (low_v, high_v, left_v, right_v),
                        early_send, early_recv)
    halo_start(early)

    def steady(i, carry):
        sample(i)
        advance(i - 1)
        spread(i - 2)
        send(i - 2)
        return carry

    lax.fori_loop(2, chunks, steady, 0)
    advance(chunks - 1)
    spread(chunks - 2)
    send(chunks - 2)
    spread(chunks - 1)
    send(chunks - 1, True)
    scatter(tile_v, [spread_v], [source_v])
    halo_here(early)
    halo_sent(early)
    fluid_v[:, pl.ds(0, width), :] = low_v[...]
    fluid_v[:, pl.ds((length + 1) * width, width), :] = high_v[...]

    def flow(s, carry):
        def store(c, new):
            new_v[c, pl.ds(pl.multiple_of(s * width, width), width), :] = new
            first_v[c, pl.ds(s, 1), :] = new[0:1]
            last_v[c, pl.ds(s, 1), :] = new[width - 1 : width]

        flow_plane(s, width, fluid_v, left_v, right_v, source_v, store)
        return carry

    lax.fori_loop(0, length, flow, 0)
    keep = pltpu.make_async_copy(new_v, fluid_out, store_sem)
    keep.start()

    def sent(n, carry):
        to_peer(n).wait_send()
        return carry

    lax.fori_loop(0, devices - 1, sent, 0)
    late = halo_copies(ends_of(new_v, 0), (first_v, last_v), (low_out, high_out, left_out, right_out),
                       late_send, late_recv)
    halo_start(late)
    zeros = [pltpu.make_async_copy(zero_v, out, zero_sems.at[n]) for n, out in enumerate((low_out, high_out))]
    pl.when(stream == 0)(zeros[0].start)
    pl.when(stream == last_stream)(zeros[1].start)
    own.wait()

    def came(n, carry):
        from_peer((me + n) % devices).wait_recv()
        return carry

    lax.fori_loop(1, devices, came, 0)
    halo_here(late)
    halo_sent(late)
    pl.when(stream == 0)(zeros[0].wait)
    pl.when(stream == last_stream)(zeros[1].wait)
    keep.wait()


def first_step(fluid, order, tiles_ids, counts, bubbles, length, width):
    streams, azims = lax.axis_size("stream"), lax.axis_size("azim")
    devices = streams * azims
    comps, tiles, cells = fluid.shape
    slots, lanes = order.shape[0], bubbles.shape[1]
    cap = slots // devices

    def out(*shape):
        return jax.ShapeDtypeStruct(shape, f32)

    def buffer(*shape):
        return pltpu.VMEM(shape, f32)

    def dma(*shape):
        return pltpu.SemaphoreType.DMA(shape)

    end, side = (comps, width, cells), (comps, length, cells)
    per_slot = buffer(slots, lanes)
    anywhere = pl.BlockSpec(memory_space=pl.ANY)
    return pl.pallas_call(
        functools.partial(first_kernel, streams, azims, cap, length, width),
        out_shape=(out(*fluid.shape), out(devices, STATES, cap, lanes),
                   out(*end), out(*end), out(*side), out(*side)),
        in_specs=[pl.BlockSpec(memory_space=pltpu.SMEM)] * 3 + [anywhere] * 2,
        out_specs=(anywhere,) * 6,
        scratch_shapes=[
            buffer(comps, tiles + 2 * width, cells), buffer(*fluid.shape),
            buffer(*end), buffer(*end), buffer(*side), buffer(*side), buffer(*side), buffer(*side),
            buffer(*end), buffer(*bubbles.shape), buffer(STATES, slots, lanes),
            per_slot, per_slot, per_slot, per_slot, per_slot, per_slot, per_slot,
            buffer(devices, STATES, cap, lanes), buffer(slots, cells), buffer(tiles, cells),
            buffer(max(cap, CHUNK) // QUAD, 16, 2 * cells),
            dma(2), dma(), dma(), dma(2), dma(devices), dma(devices), dma(4), dma(4), dma(4), dma(4),
        ],
        compiler_params=pltpu.CompilerParams(
            vmem_limit_bytes=VMEM_GRANT, collective_id=0, has_side_effects=True
        ),
        cost_estimate=pl.CostEstimate(
            flops=slots * lanes * cells * 2000, bytes_accessed=12 * 2**20,
            transcendentals=2 * slots * lanes * cells,
        ),
        name="first_step",
    )(order, tiles_ids, counts, bubbles, fluid)


def second_kernel(live_ref, tiles_ref, arrived_ref, p_ref, u_ref,
                  bubbles_out, source_ref, void_ref,
                  now_v, tile_v, amount_v, volume_v, new_v, sp, su, sn, rows_v, voids_v, lhs, list_ref):
    cells_n, lanes = p_ref.shape[-1], sp.shape[1]
    cap = arrived_ref.shape[2]
    slots = tiles_ref.shape[0]
    columns = cell_columns(cells_n, lanes)
    tiles = cells_n // 8
    clear_lhs(lhs)
    bubbles_out[...] = jnp.zeros_like(bubbles_out)
    tile_v[...] = jnp.full(tile_v.shape, -1.0, f32)
    rows_v[...] = jnp.zeros_like(rows_v)
    voids_v[...] = jnp.zeros_like(voids_v)

    def keep(i, n):
        for k in range(GROUP):
            list_ref[n] = i * GROUP + k
            n = n + live_ref[i * GROUP + k]
        return n

    number = lax.fori_loop(0, slots // GROUP, keep, 0)
    chunks = (number + CHUNK - 1) // CHUNK

    def pad(i, carry):
        list_ref[i] = list_ref[0]
        return carry

    lax.fori_loop(number, jnp.maximum(chunks, 1) * CHUNK, pad, 0)

    def sample(i):
        for q in range(CHUNK // QUAD):
            at = i * CHUNK + q * QUAD
            rows, positions = [], []
            for j in range(QUAD):
                slot = list_ref[at + j]
                tile = tiles_ref[slot]
                for c in range(STATES):
                    now_v[c, pl.ds(at + j, 1), :] = arrived_ref[slot // cap, c, pl.ds(slot % cap, 1), :]
                tile_v[pl.ds(at + j, 1), :] = jnp.full((1, lanes), tile.astype(f32), f32)
                positions.append(arrived_ref[slot // cap, 2, pl.ds(slot % cap, 1), :])
                rows.append((p_ref[0, pl.ds(tile, 1), :], u_ref[0, pl.ds(tile, 1), :]))
            sample_quad(q, at, positions, columns, lambda j: rows[j], lhs, sp, su, sn)

    def advance(i):
        for g in range(CHUNK // GROUP):
            base = pl.multiple_of(i * CHUNK + g * GROUP, GROUP)
            at = pl.ds(base, GROUP)
            state = [now_v[c, at, :] for c in range(STATES)]
            new = advance_group(state, sp[at, :], su[at, :], sn[at, :])
            live = base + lax.broadcasted_iota(jnp.int32, (GROUP, lanes), 0) < number
            amount_v[at, :] = jnp.where(live, source_amount(new[0], new[1]), 0.0)
            volume_v[at, :] = jnp.where(live, void_amount(new[0]), 0.0)
            for c in range(STATES):
                new_v[c, at, :] = new[c]

    def spread(i):
        for g in range(CHUNK // GROUP):
            base = pl.multiple_of(i * CHUNK + g * GROUP, GROUP)
            amounts = [amount_v[pl.ds(base, GROUP), :], volume_v[pl.ds(base, GROUP), :]]
            for pair in range(GROUP // 2):
                positions = [new_v[2, pl.ds(base + 2 * pair + n, 1), :] for n in range(2)]
                rows = spread_pair(pair, positions, amounts, columns, tiles)
                for n in range(2):
                    at = base + 2 * pair + n
                    rows_v[pl.ds(at, 1), :] = rows[n]
                    voids_v[pl.ds(at, 1), :] = rows[2 + n]
                    slot = list_ref[at]
                    for c in range(STATES):
                        bubbles_out[pl.ds(c * slots + slot, 1), :] = new_v[c, pl.ds(at, 1), :]

    @pl.when(number > 0)
    def _():
        sample(0)
        sample(jnp.minimum(1, chunks - 1))
        advance(0)

        def steady(i, carry):
            sample(jnp.minimum(i, chunks - 1))
            advance(i - 1)
            spread(i - 2)
            return carry

        lax.fori_loop(2, chunks + 1, steady, 0)
        spread(chunks - 1)

    scatter(tile_v, [rows_v, voids_v], [source_ref, void_ref])


def whole(shape):
    return pl.BlockSpec(tuple(shape), lambda i: (0,) * len(shape))


def bubbles_second(fluid, live, tiles_ids, arrived):
    comps, tiles, cells = fluid.shape
    slots, lanes = tiles_ids.shape[0], arrived.shape[3]

    def out(*shape):
        return jax.ShapeDtypeStruct(shape, f32)

    def buffer(*shape):
        return pltpu.VMEM(shape, f32)

    per_slot = buffer(slots, lanes)
    outs = (out(STATES * slots, lanes), out(tiles, cells), out(tiles, cells))
    return pl.pallas_call(
        second_kernel,
        grid=(1,),
        out_shape=outs,
        in_specs=[pl.BlockSpec(memory_space=pltpu.SMEM)] * 2 + [
            whole(arrived.shape),
            pl.BlockSpec((1, tiles, cells), lambda i: (0, 0, 0)),
            pl.BlockSpec((1, tiles, cells), lambda i: (comps - 1, 0, 0)),
        ],
        out_specs=tuple(whole(o.shape) for o in outs),
        scratch_shapes=[
            buffer(STATES, slots, lanes), per_slot, per_slot, per_slot, buffer(STATES, slots, lanes),
            per_slot, per_slot, per_slot, buffer(slots, cells), buffer(slots, cells),
            buffer(CHUNK // QUAD, 16, 2 * cells), pltpu.SMEM((slots + CHUNK,), jnp.int32),
        ],
        compiler_params=pltpu.CompilerParams(vmem_limit_bytes=VMEM_GRANT),
        cost_estimate=pl.CostEstimate(
            flops=slots * lanes * cells * 2000, bytes_accessed=6 * 2**20,
            transcendentals=2 * slots * lanes * cells,
        ),
        name="bubbles_second",
    )(live, tiles_ids, arrived, fluid, fluid)


def flow_kernel(f_ref, before_ref, after_ref, low_ref, high_ref, left_ref, right_ref, source_ref, out_ref, window):
    step, steps = pl.program_id(0), pl.num_programs(0)
    comps, rows, cells = f_ref.shape
    width = low_ref.shape[1]
    depth = rows // width
    window[:, pl.ds(0, width), :] = jnp.where(step == 0, low_ref[...], before_ref[...])
    window[:, pl.ds((depth + 1) * width, width), :] = jnp.where(step == steps - 1, high_ref[...], after_ref[...])
    window[:, pl.ds(width, rows), :] = f_ref[...]

    def flow(s, carry):
        def store(c, new):
            out_ref[c, pl.ds(pl.multiple_of(s * width, width), width), :] = new

        flow_plane(s, width, window, left_ref, right_ref, source_ref, store)
        return carry

    lax.fori_loop(0, depth, flow, 0)


def flow_second(fluid, low, high, left, right, source):
    comps, tiles, cells = fluid.shape
    width, length = low.shape[1], left.shape[1]
    depth = 16
    rows = depth * width
    side = pl.BlockSpec((comps, depth, cells), lambda i: (0, i, 0))
    main = pl.BlockSpec((comps, rows, cells), lambda i: (0, i, 0))
    plane = (comps, width, cells)
    return pl.pallas_call(
        flow_kernel,
        grid=(length // depth,),
        out_shape=jax.ShapeDtypeStruct(fluid.shape, f32),
        in_specs=[
            main,
            pl.BlockSpec(plane, lambda i: (0, jnp.maximum(i * depth - 1, 0), 0)),
            pl.BlockSpec(plane, lambda i: (0, jnp.minimum(i * depth + depth, length - 1), 0)),
            whole(plane), whole(plane), side, side,
            pl.BlockSpec((rows, cells), lambda i: (i, 0)),
        ],
        out_specs=main,
        scratch_shapes=[pltpu.VMEM((comps, rows + 2 * width, cells), f32)],
        compiler_params=pltpu.CompilerParams(vmem_limit_bytes=VMEM_GRANT),
        cost_estimate=pl.CostEstimate(
            flops=fluid.size * 30, bytes_accessed=10 * 2**20, transcendentals=0
        ),
        name="flow_second",
    )(fluid, fluid, fluid, low, high, left, right, source)


def on_device(fluid, bubbles, counts, outgoing_block_order, tiles_first_update, tiles_after):
    comps, length, width, cells = fluid.shape
    slots, states, lanes = bubbles.shape
    flat = (comps, length * width, cells)
    bubbles = bubbles.transpose(1, 0, 2).reshape(states * slots, lanes)
    fluid, arrived, low, high, left, right = first_step(
        fluid.reshape(flat), outgoing_block_order, tiles_first_update, counts, bubbles, length, width
    )
    live = (arrived[:, 0, :, 0] * arrived[:, 4, :, 0] >= 0.0).astype(jnp.int32).reshape(slots)
    bubbles, source, void = bubbles_second(fluid, live, tiles_after, arrived)
    fluid = flow_second(fluid, low, high, left, right, source)
    bubbles = bubbles.reshape(states, slots, lanes).transpose(1, 0, 2)
    return fluid.reshape(comps, length, width, cells), bubbles, void.reshape(length, width, cells)


def solution(mesh):
    return jax.shard_map(
        on_device,
        mesh=mesh,
        in_specs=(
            P(None, "stream", "azim", None),
            P(("stream", "azim"), None, None),
            P(("stream", "azim")),
            P(("stream", "azim")),
            P(("stream", "azim")),
            P(("stream", "azim")),
        ),
        out_specs=(
            P(None, "stream", "azim", None),
            P(("stream", "azim"), None, None),
            P("stream", "azim", None),
        ),
        check_vma=False,
    )
```

profile of v0, /device:TPU:0, one launch (start us, length us, event | category | flops | bytes accessed | tf_op | source)
XLA Modules:
  0.0 98.0 jit_solution(8943659461399805585)
XLA Ops:
  1.3 53.6 %first_step.1 = (f32[4,2048,128]{2,1,0:T(8,128)}, f32[32,5,16,128]{3,2,1,0:T(8,128)}, f32[4,32,128]{2,1,0:T(8,128)}, f32[4,32,128]{2,1,0:T(8,128)}, f32[4,64,128]{2,1,0:T(8,128)}, /*index=5*/f32[4,64,128]{2,1,0:T(8,128)}) custom-call(s32[512]{0:T(512)} %order_ref.1, s32[512]{0:T(512)} %tiles_ref.2, s32[1]{0:T(128)S(6)} %copy.9.count_ref, ...), custom_call_target="tpu_custom_call" | custom-call | flops 16777216000 | bytes 12582912 | tf_op jit(solution)/shard_map/first_step/pallas_call | solution.py:484
  54.8 1.7 %convert_reduce_fusion = s32[32,16]{1,0:T(8,128)S(1)} fusion(f32[32,5,16,128]{3,2,1,0:T(8,128)} %get-tuple-element.17.arrived_ref), kind=kLoop, calls=%fused_computation | loop fusion | flops 1536 | bytes 6144 | tf_op jit(solution)/shard_map/convert_element_type | solution.py:694
  56.5 0.7 reshape.34.live_ref
  57.2 30.9 %bubbles_second.1 = (f32[2560,128]{1,0:T(8,128)}, f32[2048,128]{1,0:T(8,128)}, f32[2048,128]{1,0:T(8,128)}) custom-call(s32[512]{0:T(512)} %reshape.34.live_ref, s32[512]{0:T(512)} %tiles_ref.3, f32[32,5,16,128]{3,2,1,0:T(8,128)} %get-tuple-element.17.arrived_ref, f32[4,2048,128]{2,1,0:T(8,128)} %get-tuple-element.12.p_ref.u_ref.f_ref.before_ref.after_ref, ...), custom_call_target="tpu_custom_call" | custom-call | flops 16777216000 | bytes 6291456 | tf_op jit(solution)/shard_map/bubbles_second/pallas_call | solution.py:614
  88.0 9.9 %flow_second.1 = f32[4,2048,128]{2,1,0:T(8,128)} custom-call(f32[4,2048,128]{2,1,0:T(8,128)} %get-tuple-element.12.p_ref.u_ref.f_ref.before_ref.after_ref, f32[4,2048,128]{2,1,0:T(8,128)} %get-tuple-element.12.p_ref.u_ref.f_ref.before_ref.after_ref, f32[4,2048,128]{2,1,0:T(8,128)} %get-tuple-element.12.p_ref.u_ref.f_ref.before_ref.after_ref, ...), custom_call_target="tpu_custom_call" | custom-call | flops 31457280 | bytes 10485760 | tf_op jit(solution)/shard_map/flow_second/pallas_call | solution.py:665
where the time goes:
time: 97 us; the launch traced here: 98 us
  Pallas kernels  94.4 us (97%)
  other arithmetic  1.66 us (2%)
  between operations  1.29 us (1%)
    pallas_call x1, Pallas kernels, first_step(): pl.pallas_call(functools.partial(first_kernel, streams, azims, cap, lengt...  53.6 us
    pallas_call x1, Pallas kernels, bubbles_second(): pl.pallas_call(second_kernel, grid=(1,), out_shape=outs, in_specs=[pl.Blo...  30.9 us
    pallas_call x1, Pallas kernels, flow_second(): pl.pallas_call(flow_kernel, grid=(length // depth,), out_shape=jax.ShapeD...  9.94 us

commit v1 on v0

v1 whole, which is shorter than its diff:
```python
import functools

import jax
import jax.numpy as jnp
from jax import lax
from jax.experimental import pallas as pl
from jax.experimental.pallas import tpu as pltpu
from jax.sharding import PartitionSpec as P

MESH = pl.DeviceIdType.MESH
SUBSTEPS = 8
TIME_STEP = 0.25
MEAN_FLOW = 0.5
DIFFUSION = 0.1
KERNEL_WIDTH = 1.5
GAS_INDEX = 4.2
PRESSURE_COUPLING = 0.3
AMBIENT = 1.0
RELAX_TIME = 0.5
VISCOUS = 0.08
SOURCE_GAIN = 0.05
VOID_SCALE = 0.01
FOUR_PI = 12.566370614359172
LOG2E = 1.4426950408889634
SHARPNESS = 0.5 * LOG2E / (KERNEL_WIDTH * KERNEL_WIDTH)
GROUP = 8
QUAD = 4
CHUNK = 16
STATES = 5
WIDE = 4
VMEM_GRANT = 60 * 2**20
f32, bf16 = jnp.float32, jnp.bfloat16


SAMPLE_SPANS = (7, 9)
SPREAD_SPANS = (5, 5, 6)


def runs(spans, tiles):
    out, start = [], 0
    while start < tiles:
        end = min(start + spans[len(out) % len(spans)], tiles)
        out.append((start, (start + end - 1) // 2, end))
        start = end
    return out


def cell_columns(cells_n, lanes):
    column = lax.broadcasted_iota(jnp.int32, (8, lanes), 0).astype(f32)
    tiles = cells_n // 8
    middles = sorted({m for spans in (SAMPLE_SPANS, SPREAD_SPANS) for _, m, _ in runs(spans, tiles)})
    return {m: column + float(8 * m) for m in middles}


def raw_weights(position, columns, tiles, spans):
    pieces = [None] * tiles
    for start, middle, end in runs(spans, tiles):
        offset = columns[middle] - position
        slope = offset * -SHARPNESS
        at = slope * offset
        pieces[middle] = jnp.exp2(at)
        for n in range(1, max(end - middle, middle - start + 1)):
            near = at - 64.0 * SHARPNESS * n * n
            step = slope * (16.0 * n)
            if middle - n >= start:
                pieces[middle - n] = jnp.exp2(near - step)
            if middle + n < end:
                pieces[middle + n] = jnp.exp2(near + step)
    return jnp.concatenate(pieces, axis=0)


def split_bf16(values):
    high = values.astype(bf16)
    low = (values - high.astype(f32)).astype(bf16)
    return high, low


def two_parts(rows):
    high = rows.astype(bf16).astype(f32)
    return jnp.concatenate([high, rows - high], axis=0).astype(bf16)


def clear_lhs(lhs):
    cells_n = lhs.shape[2] // 2
    lhs[...] = jnp.zeros_like(lhs)
    one = jnp.ones((1, cells_n), f32)
    for q in range(lhs.shape[0]):
        lhs[q, 4:5, :cells_n] = one
        lhs[q, 12:13, cells_n:] = one


def sample_quad(q, at, positions, columns, rows_of, lhs, sp, su, sn):
    cells_n = lhs.shape[2] // 2
    weights = []
    for j in range(QUAD):
        p_row, u_row = rows_of(j)
        row, side = 8 * (j // 2) + 2 * (j % 2), slice(cells_n * (j // 2), cells_n * (j // 2 + 1))
        lhs[q, row : row + 1, side] = p_row
        lhs[q, row + 1 : row + 2, side] = u_row
        weights.append(raw_weights(positions[j], columns, cells_n // 8, SAMPLE_SPANS).astype(bf16))
    rhs = jnp.concatenate(
        [jnp.concatenate(weights[:2], axis=1), jnp.concatenate(weights[2:], axis=1)], axis=0
    )
    result = jnp.dot(two_parts(lhs[q]), rhs, preferred_element_type=f32)
    result = result[:16] + result[16:]
    lanes = rhs.shape[1] // 2
    for j in range(QUAD):
        row, part = 8 * (j // 2), result[:, lanes * (j % 2) : lanes * (j % 2 + 1)]
        first = row + 2 * (j % 2)
        sp[pl.ds(at + j, 1), :] = part[first : first + 1]
        su[pl.ds(at + j, 1), :] = part[first + 1 : first + 2]
        sn[pl.ds(at + j, 1), :] = part[row + 4 : row + 5]


def drive_of(pressure, velocity, norm):
    inverse = 1.0 / norm
    return AMBIENT + PRESSURE_COUPLING * (pressure * inverse), velocity * inverse


def advance_group(radius, growth, rest, drive, substeps):
    h = TIME_STEP / SUBSTEPS
    for _ in range(substeps):
        over = 1.0 / radius
        gas = jnp.exp2((GAS_INDEX * LOG2E) * jnp.log(rest * over))
        damping = growth * (1.5 * growth + VISCOUS * over)
        growth = growth + (gas - drive - damping) * (h * over)
        radius = radius + h * growth
    return radius, growth


def travel(position, speed, velocity):
    h = TIME_STEP / SUBSTEPS
    keep = 1.0 - h / RELAX_TIME
    lag = speed - velocity
    path = h * sum(keep ** n for n in range(1, SUBSTEPS + 1))
    return position + TIME_STEP * velocity + path * lag, velocity + keep**SUBSTEPS * lag


def source_amount(radius, growth):
    return SOURCE_GAIN * FOUR_PI * radius * radius * growth


def void_amount(radius):
    return VOID_SCALE * FOUR_PI / 3.0 * radius * radius * radius


def spread_pair(pair, positions, amounts, columns, tiles):
    pieces, norms = [], []
    for position in positions:
        raw = raw_weights(position, columns, tiles, SPREAD_SPANS)
        norms.append(jnp.sum(raw, axis=0, keepdims=True))
        pieces.append(jnp.concatenate(split_bf16(raw), axis=1))
    rhs = jnp.concatenate(pieces, axis=0)
    sublane = lax.broadcasted_iota(jnp.int32, amounts[0].shape, 0)
    inverse = 1.0 / jnp.where(sublane == 2 * pair, norms[0], norms[1])
    rows = jnp.concatenate([a * inverse for a in amounts], axis=0)
    lhs = two_parts(rows)
    lhs = jnp.concatenate([lhs, lhs], axis=1)
    result = lax.dot_general(
        lhs, rhs, (((1,), (1,)), ((), ())), preferred_element_type=f32
    )
    result = result[: rows.shape[0]] + result[rows.shape[0] :]
    cells_n = 8 * tiles
    out = []
    for n in range(len(amounts)):
        for side in range(2):
            row = GROUP * n + 2 * pair + side
            out.append(result[row : row + 1, side * cells_n : (side + 1) * cells_n])
    return out


def lanes_of(rows):
    number, lanes = rows.shape
    pieces = []
    for at in range(0, number, lanes):
        block = rows[at : at + lanes]
        same = lax.broadcasted_iota(jnp.int32, block.shape, 0) == lax.broadcasted_iota(
            jnp.int32, block.shape, 1
        )
        line = jnp.sum(jnp.where(same, block, 0.0), axis=0, keepdims=True)
        pieces.append(line[:, : block.shape[0]])
    return jnp.concatenate(pieces, axis=1)


def scatter(tile_rows, parts, tiles, store):
    cells_n = parts[0].shape[1]
    ids = lanes_of(tile_rows[...])
    block = min(256, tiles)
    rhs = jnp.concatenate([x for part in parts for x in split_bf16(part[...])], axis=1)

    def some(i, carry):
        at = pl.multiple_of(i * block, block)
        tile = lax.broadcasted_iota(jnp.int32, (block, ids.shape[1]), 0) + at
        hot = jnp.where(tile.astype(f32) == ids, 1.0, 0.0).astype(bf16)
        result = jnp.dot(hot, rhs, preferred_element_type=f32)
        sums = []
        for n in range(len(parts)):
            high = result[:, 2 * n * cells_n : (2 * n + 1) * cells_n]
            sums.append(high + result[:, (2 * n + 1) * cells_n : (2 * n + 2) * cells_n])
        store(at, block, sums)
        return carry

    lax.fori_loop(0, tiles // block, some, 0)


def flow_plane(s, width, fluid, left, right, new_ref):
    comps, _, cells = fluid.shape
    row = lax.broadcasted_iota(jnp.int32, (width, cells), 0)
    lane = lax.broadcasted_iota(jnp.int32, (width, cells), 1)

    def plane(ref, c, n):
        return ref[c, pl.ds(pl.multiple_of(n * width, width), width), :]

    d_s, d_a, d_r, lap, now = [], [], [], [], []
    for c in range(comps):
        x, below, above = (plane(fluid, c, s + n) for n in (1, 0, 2))
        before = 0.0 if left is None else left[c, pl.ds(s, 1), :]
        after = 0.0 if right is None else right[c, pl.ds(s, 1), :]
        a_down = jnp.where(row == 0, before, pltpu.roll(x, 1, 0))
        a_up = jnp.where(row == width - 1, after, pltpu.roll(x, width - 1, 0))
        r_down = jnp.where(lane == 0, 0.0, pltpu.roll(x, 1, 1))
        r_up = jnp.where(lane == cells - 1, 0.0, pltpu.roll(x, cells - 1, 1))
        now.append(x)
        d_s.append(above - below)
        d_a.append(a_up - a_down)
        d_r.append(r_up - r_down)
        lap.append(above + below + a_up + a_down + r_up + r_down - 6.0 * x)
    half = 0.5 * TIME_STEP
    change = [
        MEAN_FLOW * d_s[0] + d_s[1] + d_a[2] + d_r[3],
        MEAN_FLOW * d_s[1] + d_s[0],
        MEAN_FLOW * d_s[2] + d_a[0],
        MEAN_FLOW * d_s[3] + d_r[0],
    ]
    for c in range(comps):
        at = pl.multiple_of((s + 1) * width, width)
        new_ref[c, pl.ds(at, width), :] = now[c] - half * change[c] + DIFFUSION * lap[c]


def halo_terms(side, sign, stream):
    half = sign * 0.5 * TIME_STEP
    own = DIFFUSION + (half * MEAN_FLOW if stream else 0.0)
    terms = [own * x for x in side]
    other = 1 if stream else 2
    terms[0] = terms[0] + half * side[other]
    terms[other] = terms[other] + half * side[0]
    return terms


def peer_of(n, streams, azims):
    turn, other = n // streams, n % streams
    half = azims // 2
    azim, near = lax.axis_index("azim"), turn // half
    side = (azim // half + 1 + near) % 2
    stream = (lax.axis_index("stream") + (other + 1) % streams) % streams
    return stream, side * half + (azim + turn % half + near) % half


def first_kernel(streams, azims, cap, length, width,
                 order_ref, tiles_ref, count_ref, bubbles_hbm, fluid_hbm,
                 fluid_out, rows_out, arrived, low_2, high_2, left_2, right_2,
                 fluid_v, new_v, rows_in, low_v, high_v, left_v, right_v, first_v, last_v,
                 zero_v, bubbles_v, now_v, mid_v, live_v, tile_v, amount_v, place_v, sp, su, sn, send_v, spread_v,
                 lhs, load_sems, store_sems, own_sem, send_sems, recv_sems,
                 early_send, early_recv, late_send, late_recv, zero_sems):
    devices = streams * azims
    comps, area, cells_n = fluid_hbm.shape
    slots, lanes = sp.shape
    stream, azim = lax.axis_index("stream"), lax.axis_index("azim")
    me = stream * azims + azim
    last_stream = streams - 1

    barrier = pltpu.get_barrier_semaphore()

    def greet(n, carry):
        other = (me + n) % devices
        pl.semaphore_signal(
            barrier, inc=1, device_id=(other // azims, other % azims), device_id_type=MESH
        )
        return carry

    lax.fori_loop(1, devices, greet, 0)
    inner = pl.ds(width, area)
    loads = [
        pltpu.make_async_copy(bubbles_hbm, bubbles_v, load_sems.at[0]),
        pltpu.make_async_copy(fluid_hbm.at[0], rows_in.at[0], load_sems.at[1]),
        pltpu.make_async_copy(fluid_hbm.at[comps - 1], rows_in.at[1], load_sems.at[2]),
        pltpu.make_async_copy(fluid_hbm, fluid_v.at[:, inner], load_sems.at[3]),
    ]
    for load in loads:
        load.start()
    clear_lhs(lhs)
    zero_v[...] = jnp.zeros_like(zero_v)

    @pl.when(stream == 0)
    def _():
        low_v[...] = jnp.zeros_like(low_v)

    @pl.when(stream == last_stream)
    def _():
        high_v[...] = jnp.zeros_like(high_v)

    columns = cell_columns(cells_n, lanes)
    tiles = cells_n // 8
    per = max(1, CHUNK // cap)
    chunk = per * cap
    chunks = slots // chunk
    for load in loads[:3]:
        load.wait()

    def groups(i):
        for g in range(chunk // GROUP):
            yield g, pl.ds(pl.multiple_of(i * chunk + g * GROUP, GROUP), GROUP)

    def sample(i):
        for q in range(chunk // QUAD):
            positions = []

            def rows_of(j, q=q):
                k = q * QUAD + j
                peer_stream, peer_azim = peer_of(i * per + k // cap, streams, azims)
                slot = (peer_stream * azims + peer_azim) * cap + k % cap
                block = order_ref[slot]
                tile = tiles_ref[block]
                at = i * chunk + k
                for c in range(STATES):
                    now_v[c, pl.ds(at, 1), :] = bubbles_v[pl.ds(c * slots + block, 1), :]
                live = jnp.where(block < count_ref[0], 1.0, 0.0)
                live_v[pl.ds(at, 1), :] = jnp.full((1, lanes), live, f32)
                tile_v[pl.ds(at, 1), :] = jnp.full((1, lanes), tile.astype(f32), f32)
                positions.append(bubbles_v[pl.ds(2 * slots + block, 1), :])
                return rows_in[0, pl.ds(tile, 1), :], rows_in[1, pl.ds(tile, 1), :]

            rows = [rows_of(j) for j in range(QUAD)]
            at = i * chunk + q * QUAD
            sample_quad(q, at, positions, columns, lambda j: rows[j], lhs, sp, su, sn)

    def advance_start(i):
        for g, at in groups(i):
            live = live_v[at, :] > 0.5
            state = [now_v[c, at, :] for c in range(STATES)]
            state[0] = jnp.where(live, state[0], 1.0)
            state[4] = jnp.where(live, state[4], 1.0)
            drive, velocity = drive_of(sp[at, :], su[at, :], sn[at, :])
            place, speed = travel(state[2], state[3], velocity)
            radius, growth = advance_group(state[0], state[1], state[4], drive, SUBSTEPS // 2)
            for c, x in enumerate((radius, growth, place, speed, state[4], drive)):
                mid_v[c, at, :] = x

    def advance_end(i):
        for g, at in groups(i):
            live = live_v[at, :] > 0.5
            state = [mid_v[c, at, :] for c in range(STATES + 1)]
            new = advance_group(state[0], state[1], state[4], state[5], SUBSTEPS - SUBSTEPS // 2)
            new = new + tuple(state[2:STATES])
            amount_v[at, :] = jnp.where(live, source_amount(new[0], new[1]), 0.0)
            place_v[at, :] = new[2]
            new = (jnp.where(live, new[0], -1.0),) + tuple(new[1:])
            piece = min(cap, GROUP)
            for k in range(0, GROUP, piece):
                n = g * GROUP + k
                for c in range(STATES):
                    send_v[i * per + n // cap, c, n % cap : n % cap + piece, :] = new[c][k : k + piece]

    def spread(i):
        for g in range(chunk // GROUP):
            base = pl.multiple_of(i * chunk + g * GROUP, GROUP)
            amount = amount_v[pl.ds(base, GROUP), :]
            for pair in range(GROUP // 2):
                positions = [place_v[pl.ds(base + 2 * pair + n, 1), :] for n in range(2)]
                rows = spread_pair(pair, positions, [amount], columns, tiles)
                for n in range(2):
                    spread_v[pl.ds(base + 2 * pair + n, 1), :] = rows[n]

    def to_peer(n):
        peer = peer_of(n, streams, azims)
        return pltpu.make_async_remote_copy(
            src_ref=send_v.at[n], dst_ref=arrived.at[me], send_sem=send_sems.at[n],
            recv_sem=recv_sems.at[me], device_id=peer, device_id_type=MESH,
        )

    def from_peer(other):
        return pltpu.make_async_remote_copy(
            src_ref=send_v.at[0], dst_ref=arrived.at[other], send_sem=send_sems.at[0],
            recv_sem=recv_sems.at[other], device_id=(other // azims, other % azims),
            device_id_type=MESH,
        )

    own = pltpu.make_async_copy(send_v.at[devices - 1], arrived.at[me], own_sem)

    def send(i, end=False):
        for q in range(per):
            if end and q == per - 1:
                own.start()
            else:
                to_peer(i * per + q).start()

    def halo_copies(ref, lands, sends, recvs):
        def copy(n, src, dst, peer):
            return pltpu.make_async_remote_copy(
                src_ref=src, dst_ref=dst, send_sem=sends.at[n], recv_sem=recvs.at[n],
                device_id=peer, device_id_type=MESH,
            )

        up, down = (stream + 1) % streams, (stream + streams - 1) % streams
        right, left = (azim + 1) % azims, (azim + azims - 1) % azims
        return (
            copy(0, ref.at[:, pl.ds(width * length, width)], lands[0], (up, azim)),
            copy(1, ref.at[:, pl.ds(width, width)], lands[1], (down, azim)),
            copy(2, last_v, lands[2], (stream, right)),
            copy(3, first_v, lands[3], (stream, left)),
        )

    def halo_start(copies):
        pl.when(stream < last_stream)(copies[0].start)
        pl.when(stream > 0)(copies[1].start)
        copies[2].start()
        copies[3].start()

    def halo_sent(copies):
        pl.when(stream < last_stream)(copies[0].wait_send)
        pl.when(stream > 0)(copies[1].wait_send)
        copies[2].wait_send()
        copies[3].wait_send()

    def halo_here(copies):
        pl.when(stream > 0)(copies[0].wait_recv)
        pl.when(stream < last_stream)(copies[1].wait_recv)
        copies[2].wait_recv()
        copies[3].wait_recv()

    def set_ends(ref, low, high):
        ref[:, pl.ds(0, width), :] = low
        ref[:, pl.ds((length + 1) * width, width), :] = high

    def edges(ref):
        many = 4

        def edge(n, carry):
            for k in range(many):
                s = n * many + k
                at = pl.multiple_of((s + 1) * width, width)
                for c in range(comps):
                    first_v[c, pl.ds(s, 1), :] = ref[c, pl.ds(at, 1), :]
                    last_v[c, pl.ds(s, 1), :] = ref[c, pl.ds(at + width - 1, 1), :]
            return carry

        lax.fori_loop(0, length // many, edge, 0)

    sample(0)
    loads[3].wait()
    edges(fluid_v)
    advance_start(0)
    sample(1)
    pl.semaphore_wait(barrier, devices - 1)
    early = halo_copies(fluid_v, (low_v, high_v, left_v, right_v), early_send, early_recv)
    halo_start(early)
    advance_end(0)
    advance_start(1)
    sample(2)

    def steady(i):
        spread(i - 3)
        advance_end(i - 2)
        advance_start(i - 1)
        sample(i)
        send(i - 3)

    def plain(i, carry):
        steady(i)
        return carry

    planes = 3
    begin = max(3, chunks - pl.cdiv(length, planes))
    planes = pl.cdiv(length, max(1, chunks - begin))

    def with_flow(i, carry):
        for n in range(planes):
            s = jnp.minimum((i - begin) * planes + n, length - 1)
            flow_plane(s, width, fluid_v, left_v, right_v, new_v)
        steady(i)
        return carry

    lax.fori_loop(3, begin, plain, 0)
    halo_here(early)
    set_ends(fluid_v, low_v[...], high_v[...])
    halo_sent(early)
    lax.fori_loop(begin, chunks, with_flow, 0)
    send(chunks - 3)
    spread(chunks - 3)
    advance_end(chunks - 2)
    advance_start(chunks - 1)
    send(chunks - 2)
    spread(chunks - 2)
    advance_end(chunks - 1)
    spread(chunks - 1)
    send(chunks - 1, True)

    def subtract(at, block, parts):
        rows = pl.ds(at + width, block)
        new_v[0, rows, :] = new_v[0, rows, :] - TIME_STEP * parts[0]

    scatter(tile_v, [spread_v], area, subtract)
    edges(new_v)
    late = halo_copies(new_v, (low_2, high_2, left_2, right_2), late_send, late_recv)
    keeps = [
        pltpu.make_async_copy(new_v.at[0, inner], rows_out.at[0], store_sems.at[0]),
        pltpu.make_async_copy(new_v.at[comps - 1, inner], rows_out.at[1], store_sems.at[1]),
    ]
    for keep in keeps:
        keep.start()
    halo_start(late)

    def sent(n, carry):
        to_peer(n).wait_send()
        return carry

    zeros = [pltpu.make_async_copy(zero_v, out, zero_sems.at[n]) for n, out in enumerate((low_2, high_2))]
    pl.when(stream == 0)(zeros[0].start)
    pl.when(stream == last_stream)(zeros[1].start)
    set_ends(new_v, zero_v[...], zero_v[...])
    pieces = 4
    part = length // pieces
    outs = []
    for p in range(pieces):
        def flow(n, carry, p=p):
            for k in range(4):
                flow_plane(p * part + 4 * n + k, width, new_v, None, None, fluid_v)
            return carry

        lax.fori_loop(0, part // 4, flow, 0)
        outs.append(pltpu.make_async_copy(
            fluid_v.at[:, pl.ds((p * part + 1) * width, part * width)],
            fluid_out.at[:, pl.ds(p * part * width, part * width)], store_sems.at[2 + p],
        ))
        outs[p].start()
    lax.fori_loop(0, devices - 1, sent, 0)
    own.wait()

    def came(n, carry):
        from_peer((me + n) % devices).wait_recv()
        return carry

    lax.fori_loop(1, devices, came, 0)
    halo_here(late)
    halo_sent(late)
    pl.when(stream == 0)(zeros[0].wait)
    pl.when(stream == last_stream)(zeros[1].wait)
    for copy in keeps + outs:
        copy.wait()


def shaped(*shape):
    return jax.ShapeDtypeStruct(shape, f32)


def buffer(*shape):
    return pltpu.VMEM(shape, f32)


def dma(*shape):
    return pltpu.SemaphoreType.DMA(shape)


ANYWHERE = pl.BlockSpec(memory_space=pl.ANY)
SCALARS = pl.BlockSpec(memory_space=pltpu.SMEM)


def first_step(fluid, order, tiles_ids, counts, bubbles, length, width):
    streams, azims = lax.axis_size("stream"), lax.axis_size("azim")
    devices = streams * azims
    comps, tiles, cells = fluid.shape
    slots, lanes = order.shape[0], bubbles.shape[1]
    cap = slots // devices
    end, side = buffer(comps, width, cells), buffer(comps, length, cells)
    padded = buffer(comps, tiles + 2 * width, cells)
    per_slot = buffer(slots, lanes)
    return pl.pallas_call(
        functools.partial(first_kernel, streams, azims, cap, length, width),
        out_shape=(shaped(*fluid.shape), shaped(2, tiles, cells), shaped(devices, STATES, cap, lanes),
                   *[shaped(*x.shape) for x in (end, end, side, side)]),
        in_specs=[SCALARS] * 3 + [ANYWHERE] * 2,
        out_specs=(ANYWHERE,) * 7,
        scratch_shapes=[
            padded, padded, buffer(2, tiles, cells), end, end, side, side, side, side,
            end, buffer(*bubbles.shape), buffer(STATES, slots, lanes), buffer(STATES + 1, slots, lanes),
            per_slot, per_slot, per_slot, per_slot, per_slot, per_slot, per_slot,
            buffer(devices, STATES, cap, lanes), buffer(slots, cells),
            buffer(max(cap, CHUNK) // QUAD, 16, 2 * cells),
            dma(4), dma(6), dma(), dma(devices), dma(devices), dma(4), dma(4), dma(4), dma(4), dma(2),
        ],
        compiler_params=pltpu.CompilerParams(
            vmem_limit_bytes=VMEM_GRANT, collective_id=0, has_side_effects=True
        ),
        cost_estimate=pl.CostEstimate(
            flops=slots * lanes * cells * 2000, bytes_accessed=12 * 2**20,
            transcendentals=2 * slots * lanes * cells,
        ),
        name="first_step",
    )(order, tiles_ids, counts, bubbles, fluid)


def live_list(arrived_v, devices, live_v, slots_v, rows_v):
    slots, lanes = live_v.shape
    cap = slots // devices
    for d in range(devices):
        at = d * STATES * cap
        live = arrived_v[at : at + cap, :] * arrived_v[at + 4 * cap : at + 5 * cap, :] >= 0.0
        live_v[d * cap : (d + 1) * cap, :] = jnp.where(live, 1.0, 0.0)
    live = live_v[...]
    row = lax.broadcasted_iota(jnp.int32, (slots, slots), 0)
    column = lax.broadcasted_iota(jnp.int32, (slots, slots), 1)
    before = jnp.where(column < row, 1.0, 0.0).astype(bf16)
    rank = jnp.dot(before, live.astype(bf16), preferred_element_type=f32)
    number = jnp.dot(jnp.ones((16, slots), bf16), live.astype(bf16), preferred_element_type=f32)
    rank = jnp.where(live > 0.5, rank, -1.0)
    place = lax.broadcasted_iota(jnp.int32, (slots, lanes), 1).astype(f32)
    hot = [
        jnp.where(rank - float(at) == place, 1.0, 0.0).astype(bf16)[:, : min(lanes, slots - at)]
        for at in range(0, slots, lanes)
    ]
    which = lax.broadcasted_iota(jnp.int32, (16, slots), 0)
    slot = lax.broadcasted_iota(jnp.int32, (16, slots), 1)
    digits = jnp.where(which == 0, slot // cap, slot % cap).astype(f32).astype(bf16)
    found = jnp.dot(digits, jnp.concatenate(hot, axis=1), preferred_element_type=f32)
    entry = lax.broadcasted_iota(jnp.int32, (1, slots), 1).astype(f32)
    for ref, stride in ((slots_v, cap), (rows_v, STATES * cap)):
        line = float(stride) * found[0:1] + found[1:2]
        line = jnp.where(entry < number[0:1, 0:1], line, line[:, 0:1])
        ref[:, :slots] = line.astype(jnp.int32)
        ref[:, slots:] = number[0:1].astype(jnp.int32)


def second_kernel(devices, length, tiles_ref, arrived_hbm, rows_hbm, flow_hbm, low_hbm, high_hbm, left_hbm, right_hbm, fluid_out, bubbles_out, void_out,
                  arrived_v, rows_in, flow_v, low_v, high_v, left_v, right_v, bubbles_v, void_v,
                  now_v, mid_v, fin_v, live_v, tile_v, amount_v, volume_v, sp, su, sn, rows_v, voids_v,
                  lhs, slots_v, places_v, slots_ref, places_ref, load_sems, list_sems, store_sems):
    comps, area, cells_n = flow_hbm.shape
    slots, lanes = sp.shape
    cap = slots // devices
    width = area // length
    loads = [
        pltpu.make_async_copy(arrived_hbm, arrived_v, load_sems.at[0]),
        pltpu.make_async_copy(rows_hbm, rows_in, load_sems.at[1]),
        pltpu.make_async_copy(flow_hbm, flow_v, load_sems.at[2]),
        pltpu.make_async_copy(low_hbm, low_v, load_sems.at[3]),
        pltpu.make_async_copy(high_hbm, high_v, load_sems.at[4]),
        pltpu.make_async_copy(left_hbm, left_v, load_sems.at[5]),
        pltpu.make_async_copy(right_hbm, right_v, load_sems.at[6]),
    ]
    for load in loads:
        load.start()
    columns = cell_columns(cells_n, lanes)
    tiles = cells_n // 8
    clear_lhs(lhs)
    loads[0].wait()
    live_list(arrived_v, devices, live_v, slots_v, places_v)
    lists = [
        pltpu.make_async_copy(slots_v, slots_ref, list_sems.at[0]),
        pltpu.make_async_copy(places_v, places_ref, list_sems.at[1]),
    ]
    for copy in lists:
        copy.start()
    bubbles_v[...] = jnp.zeros_like(bubbles_v)
    tile_v[...] = jnp.full(tile_v.shape, -1.0, f32)
    rows_v[...] = jnp.zeros_like(rows_v)
    voids_v[...] = jnp.zeros_like(voids_v)
    loads[1].wait()
    for copy in lists:
        copy.wait()
    number = slots_ref[0, slots]
    chunks = (number + CHUNK - 1) // CHUNK

    def groups(i):
        for g in range(CHUNK // GROUP):
            base = pl.multiple_of(i * CHUNK + g * GROUP, GROUP)
            yield base, pl.ds(base, GROUP)

    def sample(i):
        for q in range(CHUNK // QUAD):
            at = i * CHUNK + q * QUAD
            rows, positions = [], []
            for j in range(QUAD):
                place = places_ref[0, at + j]
                tile = tiles_ref[slots_ref[0, at + j]]
                for c in range(STATES):
                    now_v[c, pl.ds(at + j, 1), :] = arrived_v[pl.ds(place + c * cap, 1), :]
                tile_v[pl.ds(at + j, 1), :] = jnp.full((1, lanes), tile.astype(f32), f32)
                positions.append(arrived_v[pl.ds(place + 2 * cap, 1), :])
                rows.append((rows_in[0, pl.ds(tile, 1), :], rows_in[1, pl.ds(tile, 1), :]))
            sample_quad(q, at, positions, columns, lambda j: rows[j], lhs, sp, su, sn)

    def advance_start(i):
        for _, at in groups(i):
            state = [now_v[c, at, :] for c in range(STATES)]
            drive, velocity = drive_of(sp[at, :], su[at, :], sn[at, :])
            place, speed = travel(state[2], state[3], velocity)
            radius, growth = advance_group(state[0], state[1], state[4], drive, SUBSTEPS // 2)
            for c, x in enumerate((radius, growth, place, speed, state[4], drive)):
                mid_v[c, at, :] = x

    def advance_end(i):
        for base, at in groups(i):
            state = [mid_v[c, at, :] for c in range(STATES + 1)]
            new = advance_group(state[0], state[1], state[4], state[5], SUBSTEPS - SUBSTEPS // 2)
            new = new + tuple(state[2:STATES])
            live = base + lax.broadcasted_iota(jnp.int32, (GROUP, lanes), 0) < number
            amount_v[at, :] = jnp.where(live, source_amount(new[0], new[1]), 0.0)
            volume_v[at, :] = jnp.where(live, void_amount(new[0]), 0.0)
            for c in range(STATES):
                fin_v[c, at, :] = new[c]

    def spread(i):
        for base, rows_at in groups(i):
            amounts = [amount_v[rows_at, :], volume_v[rows_at, :]]
            for pair in range(GROUP // 2):
                positions = [fin_v[2, pl.ds(base + 2 * pair + n, 1), :] for n in range(2)]
                rows = spread_pair(pair, positions, amounts, columns, tiles)
                for n in range(2):
                    at = base + 2 * pair + n
                    rows_v[pl.ds(at, 1), :] = rows[n]
                    voids_v[pl.ds(at, 1), :] = rows[2 + n]
                    slot = slots_ref[0, at]
                    for c in range(STATES):
                        bubbles_v[pl.ds(c * slots + slot, 1), :] = fin_v[c, pl.ds(at, 1), :]

    @pl.when(number > 0)
    def _():
        def at_most(i):
            return jnp.minimum(i, chunks - 1)

        def before_end(n):
            return jnp.maximum(chunks - n, 0)

        sample(0)
        advance_start(0)
        sample(at_most(1))
        advance_end(0)
        advance_start(at_most(1))
        sample(at_most(2))

        def steady(i, carry):
            spread(i - 3)
            advance_end(i - 2)
            advance_start(i - 1)
            sample(i)
            return carry

        lax.fori_loop(3, chunks, steady, 0)
        spread(before_end(3))
        advance_end(before_end(2))
        advance_start(before_end(1))
        spread(before_end(2))
        advance_end(before_end(1))
        spread(before_end(1))

    def store(n, src, dst):
        copy = pltpu.make_async_copy(src, dst, store_sems.at[n])
        copy.start()
        return copy

    for load in loads[2:]:
        load.wait()
    first, last = pl.ds(0, width), pl.ds(area - width, width)
    begin, end = pl.ds(0, length, stride=width), pl.ds(width - 1, length, stride=width)
    for rows, ref, sign, stream in (
        (first, low_v, 1, True), (last, high_v, -1, True), (begin, left_v, 1, False), (end, right_v, -1, False)
    ):
        for c, term in enumerate(halo_terms([ref[c] for c in range(comps)], sign, stream)):
            flow_v[c, rows, :] = flow_v[c, rows, :] + term
    rest = pl.ds(1, comps - 1)
    stores = [store(0, bubbles_v, bubbles_out), store(1, flow_v.at[rest], fluid_out.at[rest])]

    def finish(at, block, parts):
        rows = pl.ds(at, block)
        flow_v[0, rows, :] = flow_v[0, rows, :] - TIME_STEP * parts[0]
        void_v[rows, :] = parts[1]

    scatter(tile_v, [rows_v, voids_v], area, finish)
    stores += [store(2, flow_v.at[0], fluid_out.at[0]), store(3, void_v, void_out)]
    for copy in stores:
        copy.wait()


def second_step(tiles_ids, arrived, rows, flow, halos):
    comps, tiles, cells = flow.shape
    slots, lanes = tiles_ids.shape[0], arrived.shape[3]
    devices, length = arrived.shape[0], halos[2].shape[1]
    arrived = arrived.reshape(slots * STATES, lanes)
    per_slot = buffer(slots, lanes)
    return pl.pallas_call(
        functools.partial(second_kernel, devices, length),
        out_shape=(shaped(*flow.shape), shaped(STATES * slots, lanes), shaped(tiles, cells)),
        in_specs=[SCALARS] + [ANYWHERE] * 7,
        out_specs=(ANYWHERE,) * 3,
        scratch_shapes=[
            buffer(*arrived.shape), buffer(*rows.shape), buffer(*flow.shape),
            *[buffer(*x.shape) for x in halos],
            buffer(STATES * slots, lanes), buffer(tiles, cells),
            buffer(STATES, slots, lanes), buffer(STATES + 1, slots, lanes), buffer(STATES, slots, lanes),
            per_slot, per_slot, per_slot, per_slot, per_slot, per_slot, per_slot,
            buffer(slots, cells), buffer(slots, cells),
            buffer(CHUNK // QUAD, 16, 2 * cells),
            *[space((1, slots + lanes), jnp.int32) for space in (pltpu.VMEM, pltpu.VMEM, pltpu.SMEM, pltpu.SMEM)],
            dma(7), dma(2), dma(4),
        ],
        compiler_params=pltpu.CompilerParams(vmem_limit_bytes=VMEM_GRANT),
        cost_estimate=pl.CostEstimate(
            flops=slots * lanes * cells * 2000, bytes_accessed=6 * 2**20,
            transcendentals=2 * slots * lanes * cells,
        ),
        name="second_step",
    )(tiles_ids, arrived, rows, flow, *halos)


def on_device(fluid, bubbles, counts, outgoing_block_order, tiles_first_update, tiles_after):
    comps, length, width, cells = fluid.shape
    slots, states, lanes = bubbles.shape
    flat = (comps, length * width, cells)
    bubbles = bubbles.transpose(1, 0, 2).reshape(states * slots, lanes)
    flow, rows, arrived, *halos = first_step(
        fluid.reshape(flat), outgoing_block_order, tiles_first_update, counts, bubbles, length, width
    )
    fluid, bubbles, void = second_step(tiles_after, arrived, rows, flow, halos)
    bubbles = bubbles.reshape(states, slots, lanes).transpose(1, 0, 2)
    return fluid.reshape(comps, length, width, cells), bubbles, void.reshape(length, width, cells)


def solution(mesh):
    return jax.shard_map(
        on_device,
        mesh=mesh,
        in_specs=(
            P(None, "stream", "azim", None),
            P(("stream", "azim"), None, None),
            P(("stream", "azim")),
            P(("stream", "azim")),
            P(("stream", "azim")),
            P(("stream", "azim")),
        ),
        out_specs=(
            P(None, "stream", "azim", None),
            P(("stream", "azim"), None, None),
            P("stream", "azim", None),
        ),
        check_vma=False,
    )
```

time: 97 us -> 70.5 us (0.73)
  the two profiles are of different devices: /device:TPU:0 before, /device:TPU:14 now
where the time goes in v1:
time: 70.5 us; the launch traced here: 70 us
  Pallas kernels  68.7 us (97%)
  between operations  1.28 us (2%)
    pallas_call x1, Pallas kernels, first_step(): pl.pallas_call(functools.partial(first_kernel, streams, azims, cap, lengt...  48.4 us
    pallas_call x1, Pallas kernels, second_step(): pl.pallas_call(functools.partial(second_kernel, devices, length), out_sha...  20.3 us

profile of v1, /device:TPU:14, one launch (start us, length us, event | category | flops | bytes accessed | tf_op | source)
XLA Modules:
  0.0 70.0 jit_solution(17747473827011112488)
XLA Ops:
  1.3 48.4 %first_step.1 = (f32[4,2048,128]{2,1,0:T(8,128)}, f32[2,2048,128]{2,1,0:T(8,128)}, f32[32,5,16,128]{3,2,1,0:T(8,128)}, f32[4,32,128]{2,1,0:T(8,128)}, f32[4,32,1...) custom-call(s32[512]{0:T(512)} %order_ref.1, s32[512]{0:T(512)} %tiles_ref.2, s32[1]{0:T(128)S(6)} %copy.9.count_ref, ...), custom_call_target="tpu_custom_call" | custom-call | flops 16777216000 | bytes 12582912 | tf_op jit(solution)/shard_map/first_step/pallas_call | solution.py:578
  49.7 20.3 %second_step.1 = (f32[4,2048,128]{2,1,0:T(8,128)}, f32[2560,128]{1,0:T(8,128)}, f32[2048,128]{1,0:T(8,128)}) custom-call(s32[512]{0:T(512)} %tiles_ref.3, f32[2560,128]{1,0:T(8,128)} %bitcast.14, f32[2,2048,128]{2,1,0:T(8,128)} %get-tuple-element.14.rows_hbm, f32[4,2048,128]{2,1,0:T(8,128)} %get-tuple-element.15.flow_hbm, ...), custom_call_target="tpu_custom_call" | custom-call | flops 16777216000 | bytes 6291456 | tf_op jit(solution)/shard_map/second_step/pallas_call | solution.py:791

commit v2 on v1

--- a/solution.py
+++ b/solution.py
@@ -169,6 +169,36 @@
     return out
 
 
+def spread_quad(quad, positions, amounts, columns, tiles):
+    weights, norms = [], []
+    for position in positions:
+        raw = raw_weights(position, columns, tiles, SPREAD_SPANS)
+        norms.append(jnp.sum(raw, axis=0, keepdims=True))
+        weights.append(raw.astype(bf16))
+    rhs = jnp.concatenate(
+        [jnp.concatenate(weights[0::2], axis=1), jnp.concatenate(weights[1::2], axis=1)], axis=0
+    )
+    row = lax.broadcasted_iota(jnp.int32, amounts.shape, 0) % QUAD
+    norm = jnp.where(
+        row < 2, jnp.where(row == 0, norms[0], norms[1]), jnp.where(row == 2, norms[2], norms[3])
+    )
+    parts = two_parts(amounts / norm)
+    none = jnp.zeros_like(parts)
+    lhs = jnp.concatenate(
+        [jnp.concatenate([parts, none], axis=1), jnp.concatenate([none, parts], axis=1)], axis=0
+    )
+    result = lax.dot_general(
+        lhs, rhs, (((1,), (1,)), ((), ())), preferred_element_type=f32
+    )
+    size, cells_n = amounts.shape[0], 8 * tiles
+    out = []
+    for j in range(QUAD):
+        first = (j // 2) * 2 * size + QUAD * quad + j
+        side = slice((j % 2) * cells_n, (j % 2 + 1) * cells_n)
+        out.append(result[first : first + 1, side] + result[first + size : first + size + 1, side])
+    return out
+
+
 def lanes_of(rows):
     number, lanes = rows.shape
     pieces = []
@@ -203,7 +233,7 @@
     lax.fori_loop(0, tiles // block, some, 0)
 
 
-def flow_plane(s, width, fluid, left, right, new_ref):
+def flow_plane(s, width, fluid, new_ref):
     comps, _, cells = fluid.shape
     row = lax.broadcasted_iota(jnp.int32, (width, cells), 0)
     lane = lax.broadcasted_iota(jnp.int32, (width, cells), 1)
@@ -214,10 +244,8 @@
     d_s, d_a, d_r, lap, now = [], [], [], [], []
     for c in range(comps):
         x, below, above = (plane(fluid, c, s + n) for n in (1, 0, 2))
-        before = 0.0 if left is None else left[c, pl.ds(s, 1), :]
-        after = 0.0 if right is None else right[c, pl.ds(s, 1), :]
-        a_down = jnp.where(row == 0, before, pltpu.roll(x, 1, 0))
-        a_up = jnp.where(row == width - 1, after, pltpu.roll(x, width - 1, 0))
+        a_down = jnp.where(row == 0, 0.0, pltpu.roll(x, 1, 0))
+        a_up = jnp.where(row == width - 1, 0.0, pltpu.roll(x, width - 1, 0))
         r_down = jnp.where(lane == 0, 0.0, pltpu.roll(x, 1, 1))
         r_up = jnp.where(lane == cells - 1, 0.0, pltpu.roll(x, cells - 1, 1))
         now.append(x)
@@ -247,21 +275,43 @@
     return terms
 
 
+def add_halos(ref, start, length, width, low, high, left, right):
+    comps = ref.shape[0]
+    for at, number, stride, side, sign in (
+        (start, width, 1, low, 1), (start + (length - 1) * width, width, 1, high, -1),
+        (start, length, width, left, 1), (start + width - 1, length, width, right, -1),
+    ):
+        rows = pl.ds(at, number) if stride == 1 else pl.ds(at, number, stride=stride)
+        terms = halo_terms([side[c] for c in range(comps)], sign, stride == 1)
+        terms = [ref[c, rows, :] + term for c, term in enumerate(terms)]
+        for c, term in enumerate(terms):
+            ref[c, rows, :] = term
+
+
 def peer_of(n, streams, azims):
     turn, other = n // streams, n % streams
-    half = azims // 2
-    azim, near = lax.axis_index("azim"), turn // half
-    side = (azim // half + 1 + near) % 2
+    step = (turn + 1) // 2 * (2 * (turn % 2) - 1)
+    away = (azims // 2 + step + azims) % azims
     stream = (lax.axis_index("stream") + (other + 1) % streams) % streams
-    return stream, side * half + (azim + turn % half + near) % half
-
-
-def first_kernel(streams, azims, cap, length, width,
-                 order_ref, tiles_ref, count_ref, bubbles_hbm, fluid_hbm,
+    return stream, (lax.axis_index("azim") + away) % azims
+
+
+def source_of(n, streams, azims):
+    turn, other = n // streams, n % streams
+    step = (turn + 1) // 2 * (2 * (turn % 2) - 1)
+    away = (azims // 2 + step + azims) % azims
+    stream = (lax.axis_index("stream") + streams - (other + 1) % streams) % streams
+    return stream * azims + (lax.axis_index("azim") + azims - away) % azims
+
+
+def first_kernel(streams, azims, cap, length, width, soon,
+                 order_ref, tiles_ref, after_ref, count_ref, bubbles_hbm, fluid_hbm,
                  fluid_out, rows_out, arrived, low_2, high_2, left_2, right_2,
+                 bubbles_out, spread_out, void_out, tile_out,
                  fluid_v, new_v, rows_in, low_v, high_v, left_v, right_v, first_v, last_v,
                  zero_v, bubbles_v, now_v, mid_v, live_v, tile_v, amount_v, place_v, sp, su, sn, send_v, spread_v,
-                 lhs, load_sems, store_sems, own_sem, send_sems, recv_sems,
+                 soon_v, dead_v, fin_v, volume_v, void_v,
+                 lhs, load_sems, store_sems, own_sem, dead_sems, send_sems, recv_sems,
                  early_send, early_recv, late_send, late_recv, zero_sems):
     devices = streams * azims
     comps, area, cells_n = fluid_hbm.shape
@@ -287,7 +337,7 @@
         pltpu.make_async_copy(fluid_hbm.at[comps - 1], rows_in.at[1], load_sems.at[2]),
         pltpu.make_async_copy(fluid_hbm, fluid_v.at[:, inner], load_sems.at[3]),
     ]
-    for load in loads:
+    for load in loads[:3]:
         load.start()
     clear_lhs(lhs)
     zero_v[...] = jnp.zeros_like(zero_v)
@@ -307,6 +357,7 @@
     chunks = slots // chunk
     for load in loads[:3]:
         load.wait()
+    loads[3].start()
 
     def groups(i):
         for g in range(chunk // GROUP):
@@ -366,25 +417,31 @@
         for g in range(chunk // GROUP):
             base = pl.multiple_of(i * chunk + g * GROUP, GROUP)
             amount = amount_v[pl.ds(base, GROUP), :]
-            for pair in range(GROUP // 2):
-                positions = [place_v[pl.ds(base + 2 * pair + n, 1), :] for n in range(2)]
-                rows = spread_pair(pair, positions, [amount], columns, tiles)
-                for n in range(2):
-                    spread_v[pl.ds(base + 2 * pair + n, 1), :] = rows[n]
-
-    def to_peer(n):
+            for quad in range(GROUP // QUAD):
+                positions = [place_v[pl.ds(base + QUAD * quad + n, 1), :] for n in range(QUAD)]
+                rows = spread_quad(quad, positions, amount, columns, tiles)
+                for n in range(QUAD):
+                    spread_v[pl.ds(base + QUAD * quad + n, 1), :] = rows[n]
+
+    def to_peer(n, place):
         peer = peer_of(n, streams, azims)
         return pltpu.make_async_remote_copy(
-            src_ref=send_v.at[n], dst_ref=arrived.at[me], send_sem=send_sems.at[n],
-            recv_sem=recv_sems.at[me], device_id=peer, device_id_type=MESH,
+            src_ref=send_v.at[n], dst_ref=place, send_sem=send_sems.at[n],
+            recv_sem=recv_sems.at[n], device_id=peer, device_id_type=MESH,
         )
 
-    def from_peer(other):
-        return pltpu.make_async_remote_copy(
-            src_ref=send_v.at[0], dst_ref=arrived.at[other], send_sem=send_sems.at[0],
-            recv_sem=recv_sems.at[other], device_id=(other // azims, other % azims),
-            device_id_type=MESH,
-        )
+    def start_to(n):
+        pl.when(n < soon)(to_peer(n, soon_v.at[jnp.minimum(n, soon - 1)]).start)
+        pl.when(n >= soon)(to_peer(n, arrived.at[me]).start)
+
+    def dead(n):
+        return pltpu.make_async_copy(dead_v, arrived.at[source_of(n, streams, azims)], dead_sems.at[n])
+
+    def wait_soon(n):
+        to_peer(n, soon_v.at[n]).wait_recv()
+
+    def wait_late(n):
+        to_peer(n, arrived.at[source_of(n, streams, azims)]).wait_recv()
 
     own = pltpu.make_async_copy(send_v.at[devices - 1], arrived.at[me], own_sem)
 
@@ -393,7 +450,7 @@
             if end and q == per - 1:
                 own.start()
             else:
-                to_peer(i * per + q).start()
+                start_to(i * per + q)
 
     def halo_copies(ref, lands, sends, recvs):
         def copy(n, src, dst, peer):
@@ -447,6 +504,9 @@
 
         lax.fori_loop(0, length // many, edge, 0)
 
+    state_row = lax.broadcasted_iota(jnp.int32, dead_v.shape, 0)
+    dead_v[...] = jnp.where(state_row == 0, -1.0, 1.0)
+    fin_v[...] = jnp.zeros_like(fin_v)
     sample(0)
     loads[3].wait()
     edges(fluid_v)
@@ -455,6 +515,12 @@
     pl.semaphore_wait(barrier, devices - 1)
     early = halo_copies(fluid_v, (low_v, high_v, left_v, right_v), early_send, early_recv)
     halo_start(early)
+
+    def bury(n, carry):
+        dead(n).start()
+        return carry
+
+    lax.fori_loop(0, soon, bury, 0)
     advance_end(0)
     advance_start(1)
     sample(2)
@@ -477,14 +543,12 @@
     def with_flow(i, carry):
         for n in range(planes):
             s = jnp.minimum((i - begin) * planes + n, length - 1)
-            flow_plane(s, width, fluid_v, left_v, right_v, new_v)
+            flow_plane(s, width, fluid_v, new_v)
         steady(i)
         return carry
 
+    set_ends(fluid_v, zero_v[...], zero_v[...])
     lax.fori_loop(3, begin, plain, 0)
-    halo_here(early)
-    set_ends(fluid_v, low_v[...], high_v[...])
-    halo_sent(early)
     lax.fori_loop(begin, chunks, with_flow, 0)
     send(chunks - 3)
     spread(chunks - 3)
@@ -496,6 +560,10 @@
     spread(chunks - 1)
     send(chunks - 1, True)
 
+    halo_here(early)
+    halo_sent(early)
+    add_halos(new_v, width, length, width, low_v, high_v, left_v, right_v)
+
     def subtract(at, block, parts):
         rows = pl.ds(at + width, block)
         new_v[0, rows, :] = new_v[0, rows, :] - TIME_STEP * parts[0]
@@ -512,7 +580,7 @@
     halo_start(late)
 
     def sent(n, carry):
-        to_peer(n).wait_send()
+        to_peer(n, soon_v.at[0]).wait_send()
         return carry
 
     zeros = [pltpu.make_async_copy(zero_v, out, zero_sems.at[n]) for n, out in enumerate((low_2, high_2))]
@@ -525,7 +593,7 @@
     for p in range(pieces):
         def flow(n, carry, p=p):
             for k in range(4):
-                flow_plane(p * part + 4 * n + k, width, new_v, None, None, fluid_v)
+                flow_plane(p * part + 4 * n + k, width, new_v, fluid_v)
             return carry
 
         lax.fori_loop(0, part // 4, flow, 0)
@@ -534,14 +602,118 @@
             fluid_out.at[:, pl.ds(p * part * width, part * width)], store_sems.at[2 + p],
         ))
         outs[p].start()
+    def peers(i):
+        for q in range(per):
+            yield q, i * per + q
+
+    def arrive(i):
+        for _, n in peers(i):
+            wait_soon(n)
+
+    def sample_2(i):
+        for q in range(chunk // QUAD):
+            rows, positions = [], []
+            for j in range(QUAD):
+                k = q * QUAD + j
+                n = i * per + k // cap
+                tile = after_ref[source_of(n, streams, azims) * cap + k % cap]
+                tile_v[pl.ds(i * chunk + k, 1), :] = jnp.full((1, lanes), tile.astype(f32), f32)
+                positions.append(soon_v[n, 2, pl.ds(k % cap, 1), :])
+                row = pl.ds(tile + width, 1)
+                rows.append((new_v[0, row, :], new_v[comps - 1, row, :]))
+            sample_quad(q, i * chunk + q * QUAD, positions, columns, lambda j: rows[j], lhs, sp, su, sn)
+
+    def state_2(i, g):
+        piece = min(cap, GROUP)
+        parts = []
+        for k in range(g * GROUP, (g + 1) * GROUP, piece):
+            parts.append([soon_v[i * per + k // cap, c, k % cap : k % cap + piece, :] for c in range(STATES)])
+        state = [x[0] if len(parts) == 1 else jnp.concatenate(x, axis=0) for x in zip(*parts)]
+        return state, state[0] * state[4] >= 0.0
+
+    def advance_start_2(i):
+        for g, at in groups(i):
+            state, live = state_2(i, g)
+            radius, rest = (jnp.where(live, x, 1.0) for x in (state[0], state[4]))
+            drive, velocity = drive_of(sp[at, :], su[at, :], sn[at, :])
+            place, speed = travel(state[2], state[3], velocity)
+            radius, growth = advance_group(radius, state[1], rest, drive, SUBSTEPS // 2)
+            for c, x in enumerate((radius, growth, place, speed, rest, drive)):
+                mid_v[c, at, :] = x
+
+    def advance_end_2(i):
+        for g, at in groups(i):
+            live = state_2(i, g)[1]
+            state = [mid_v[c, at, :] for c in range(STATES + 1)]
+            new = advance_group(state[0], state[1], state[4], state[5], SUBSTEPS - SUBSTEPS // 2)
+            new = new + tuple(state[2:STATES])
+            amount_v[at, :] = jnp.where(live, source_amount(new[0], new[1]), 0.0)
+            volume_v[at, :] = jnp.where(live, void_amount(new[0]), 0.0)
+            place_v[at, :] = new[2]
+            piece = min(cap, GROUP)
+            for k in range(0, GROUP, piece):
+                m = g * GROUP + k
+                source = source_of(i * per + m // cap, streams, azims)
+                for c in range(STATES):
+                    fin_v[c, source, m % cap : m % cap + piece, :] = jnp.where(live, new[c], 0.0)[k : k + piece]
+
+    def spread_2(i):
+        for g, at in groups(i):
+            base = i * chunk + g * GROUP
+            amounts = [amount_v[at, :], volume_v[at, :]]
+            for pair in range(GROUP // 2):
+                positions = [place_v[pl.ds(base + 2 * pair + n, 1), :] for n in range(2)]
+                rows = spread_pair(pair, positions, amounts, columns, tiles)
+                for n in range(2):
+                    spread_v[pl.ds(base + 2 * pair + n, 1), :] = rows[n]
+                    void_v[pl.ds(base + 2 * pair + n, 1), :] = rows[2 + n]
+
+    count = soon // per
+    arrive(0)
+    sample_2(0)
+    arrive(1)
+    advance_start_2(0)
+    sample_2(1)
+    arrive(2)
+    advance_end_2(0)
+    advance_start_2(1)
+    sample_2(2)
+
+    def steady_2(i, carry):
+        arrive(i)
+        spread_2(i - 3)
+        advance_end_2(i - 2)
+        advance_start_2(i - 1)
+        sample_2(i)
+        return carry
+
+    lax.fori_loop(3, count, steady_2, 0)
+    spread_2(count - 3)
+    advance_end_2(count - 2)
+    advance_start_2(count - 1)
+    spread_2(count - 2)
+    advance_end_2(count - 1)
+    spread_2(count - 1)
+    done = pl.ds(0, soon * cap)
+    for n, (src, dst) in enumerate((
+        (fin_v, bubbles_out), (spread_v.at[done], spread_out), (void_v, void_out), (tile_v.at[done], tile_out)
+    )):
+        outs.append(pltpu.make_async_copy(src, dst, store_sems.at[2 + pieces + n]))
+        outs[-1].start()
     lax.fori_loop(0, devices - 1, sent, 0)
     own.wait()
 
     def came(n, carry):
-        from_peer((me + n) % devices).wait_recv()
+        wait_late(n)
         return carry
 
-    lax.fori_loop(1, devices, came, 0)
+    lax.fori_loop(soon, devices - 1, came, 0)
+
+    def buried(n, carry):
+        dead(n).wait()
+        return carry
+
+    lax.fori_loop(0, soon, buried, 0)
     halo_here(late)
     halo_sent(late)
     pl.when(stream == 0)(zeros[0].wait)
@@ -566,28 +738,32 @@
 SCALARS = pl.BlockSpec(memory_space=pltpu.SMEM)
 
 
-def first_step(fluid, order, tiles_ids, counts, bubbles, length, width):
+def first_step(fluid, order, tiles_ids, after_ids, counts, bubbles, length, width):
     streams, azims = lax.axis_size("stream"), lax.axis_size("azim")
     devices = streams * azims
     comps, tiles, cells = fluid.shape
     slots, lanes = order.shape[0], bubbles.shape[1]
     cap = slots // devices
+    soon = 3 * devices // 8
     end, side = buffer(comps, width, cells), buffer(comps, length, cells)
     padded = buffer(comps, tiles + 2 * width, cells)
     per_slot = buffer(slots, lanes)
     return pl.pallas_call(
-        functools.partial(first_kernel, streams, azims, cap, length, width),
+        functools.partial(first_kernel, streams, azims, cap, length, width, soon),
         out_shape=(shaped(*fluid.shape), shaped(2, tiles, cells), shaped(devices, STATES, cap, lanes),
-                   *[shaped(*x.shape) for x in (end, end, side, side)]),
-        in_specs=[SCALARS] * 3 + [ANYWHERE] * 2,
-        out_specs=(ANYWHERE,) * 7,
+                   *[shaped(*x.shape) for x in (end, end, side, side)],
+                   shaped(STATES, devices, cap, lanes), *[shaped(soon * cap, cells)] * 2, shaped(soon * cap, lanes)),
+        in_specs=[SCALARS] * 4 + [ANYWHERE] * 2,
+        out_specs=(ANYWHERE,) * 11,
         scratch_shapes=[
             padded, padded, buffer(2, tiles, cells), end, end, side, side, side, side,
             end, buffer(*bubbles.shape), buffer(STATES, slots, lanes), buffer(STATES + 1, slots, lanes),
             per_slot, per_slot, per_slot, per_slot, per_slot, per_slot, per_slot,
             buffer(devices, STATES, cap, lanes), buffer(slots, cells),
+            buffer(soon, STATES, cap, lanes), buffer(STATES, cap, lanes), buffer(STATES, devices, cap, lanes),
+            per_slot, buffer(soon * cap, cells),
             buffer(max(cap, CHUNK) // QUAD, 16, 2 * cells),
-            dma(4), dma(6), dma(), dma(devices), dma(devices), dma(4), dma(4), dma(4), dma(4), dma(2),
+            dma(4), dma(10), dma(), dma(soon), dma(devices), dma(devices), dma(4), dma(4), dma(4), dma(4), dma(2),
         ],
         compiler_params=pltpu.CompilerParams(
             vmem_limit_bytes=VMEM_GRANT, collective_id=0, has_side_effects=True
@@ -597,7 +773,7 @@
             transcendentals=2 * slots * lanes * cells,
         ),
         name="first_step",
-    )(order, tiles_ids, counts, bubbles, fluid)
+    )(order, tiles_ids, after_ids, counts, bubbles, fluid)
 
 
 def live_list(arrived_v, devices, live_v, slots_v, rows_v):
@@ -631,7 +807,8 @@
         ref[:, slots:] = number[0:1].astype(jnp.int32)
 
 
-def second_kernel(devices, length, tiles_ref, arrived_hbm, rows_hbm, flow_hbm, low_hbm, high_hbm, left_hbm, right_hbm, fluid_out, bubbles_out, void_out,
+def second_kernel(devices, length, tiles_ref, arrived_hbm, rows_hbm, flow_hbm, low_hbm, high_hbm, left_hbm, right_hbm,
+                  bubbles_hbm, spread_hbm, spread_void_hbm, spread_tile_hbm, fluid_out, bubbles_out, void_out,
                   arrived_v, rows_in, flow_v, low_v, high_v, left_v, right_v, bubbles_v, void_v,
                   now_v, mid_v, fin_v, live_v, tile_v, amount_v, volume_v, sp, su, sn, rows_v, voids_v,
                   lhs, slots_v, places_v, slots_ref, places_ref, load_sems, list_sems, store_sems):
@@ -639,6 +816,8 @@
     slots, lanes = sp.shape
     cap = slots // devices
     width = area // length
+    ahead = slots - spread_hbm.shape[0]
+    behind = pl.ds(ahead, slots - ahead)
     loads = [
         pltpu.make_async_copy(arrived_hbm, arrived_v, load_sems.at[0]),
         pltpu.make_async_copy(rows_hbm, rows_in, load_sems.at[1]),
@@ -647,6 +826,10 @@
         pltpu.make_async_copy(high_hbm, high_v, load_sems.at[4]),
         pltpu.make_async_copy(left_hbm, left_v, load_sems.at[5]),
         pltpu.make_async_copy(right_hbm, right_v, load_sems.at[6]),
+        pltpu.make_async_copy(bubbles_hbm, bubbles_v, load_sems.at[7]),
+        pltpu.make_async_copy(spread_hbm, rows_v.at[behind], load_sems.at[8]),
+        pltpu.make_async_copy(spread_void_hbm, voids_v.at[behind], load_sems.at[9]),
+        pltpu.make_async_copy(spread_tile_hbm, tile_v.at[behind], load_sems.at[10]),
     ]
     for load in loads:
         load.start()
@@ -661,11 +844,11 @@
     ]
     for copy in lists:
         copy.start()
-    bubbles_v[...] = jnp.zeros_like(bubbles_v)
-    tile_v[...] = jnp.full(tile_v.shape, -1.0, f32)
-    rows_v[...] = jnp.zeros_like(rows_v)
-    voids_v[...] = jnp.zeros_like(voids_v)
-    loads[1].wait()
+    tile_v[:ahead, :] = jnp.full((ahead, lanes), -1.0, f32)
+    rows_v[:ahead, :] = jnp.zeros((ahead, cells_n), f32)
+    voids_v[:ahead, :] = jnp.zeros((ahead, cells_n), f32)
+    for load in (loads[1], *loads[7:]):
+        load.wait()
     for copy in lists:
         copy.wait()
     number = slots_ref[0, slots]
@@ -759,15 +942,9 @@
         copy.start()
         return copy
 
-    for load in loads[2:]:
+    for load in loads[2:7]:
         load.wait()
-    first, last = pl.ds(0, width), pl.ds(area - width, width)
-    begin, end = pl.ds(0, length, stride=width), pl.ds(width - 1, length, stride=width)
-    for rows, ref, sign, stream in (
-        (first, low_v, 1, True), (last, high_v, -1, True), (begin, left_v, 1, False), (end, right_v, -1, False)
-    ):
-        for c, term in enumerate(halo_terms([ref[c] for c in range(comps)], sign, stream)):
-            flow_v[c, rows, :] = flow_v[c, rows, :] + term
+    add_halos(flow_v, 0, length, width, low_v, high_v, left_v, right_v)
     rest = pl.ds(1, comps - 1)
     stores = [store(0, bubbles_v, bubbles_out), store(1, flow_v.at[rest], fluid_out.at[rest])]
 
@@ -782,7 +959,7 @@
         copy.wait()
 
 
-def second_step(tiles_ids, arrived, rows, flow, halos):
+def second_step(tiles_ids, arrived, rows, flow, halos, bubbles, parts):
     comps, tiles, cells = flow.shape
     slots, lanes = tiles_ids.shape[0], arrived.shape[3]
     devices, length = arrived.shape[0], halos[2].shape[1]
@@ -791,7 +968,7 @@
     return pl.pallas_call(
         functools.partial(second_kernel, devices, length),
         out_shape=(shaped(*flow.shape), shaped(STATES * slots, lanes), shaped(tiles, cells)),
-        in_specs=[SCALARS] + [ANYWHERE] * 7,
+        in_specs=[SCALARS] + [ANYWHERE] * 11,
         out_specs=(ANYWHERE,) * 3,
         scratch_shapes=[
             buffer(*arrived.shape), buffer(*rows.shape), buffer(*flow.shape),
@@ -802,7 +979,7 @@
             buffer(slots, cells), buffer(slots, cells),
             buffer(CHUNK // QUAD, 16, 2 * cells),
             *[space((1, slots + lanes), jnp.int32) for space in (pltpu.VMEM, pltpu.VMEM, pltpu.SMEM, pltpu.SMEM)],
-            dma(7), dma(2), dma(4),
+            dma(11), dma(2), dma(4),
         ],
         compiler_params=pltpu.CompilerParams(vmem_limit_bytes=VMEM_GRANT),
         cost_estimate=pl.CostEstimate(
@@ -810,7 +987,7 @@
             transcendentals=2 * slots * lanes * cells,
         ),
         name="second_step",
-    )(tiles_ids, arrived, rows, flow, *halos)
+    )(tiles_ids, arrived, rows, flow, *halos, bubbles.reshape(STATES * slots, lanes), *parts)
 
 
 def on_device(fluid, bubbles, counts, outgoing_block_order, tiles_first_update, tiles_after):
@@ -818,10 +995,10 @@
     slots, states, lanes = bubbles.shape
     flat = (comps, length * width, cells)
     bubbles = bubbles.transpose(1, 0, 2).reshape(states * slots, lanes)
-    flow, rows, arrived, *halos = first_step(
-        fluid.reshape(flat), outgoing_block_order, tiles_first_update, counts, bubbles, length, width
+    flow, rows, arrived, *rest = first_step(
+        fluid.reshape(flat), outgoing_block_order, tiles_first_update, tiles_after, counts, bubbles, length, width
     )
-    fluid, bubbles, void = second_step(tiles_after, arrived, rows, flow, halos)
+    fluid, bubbles, void = second_step(tiles_after, arrived, rows, flow, rest[:4], rest[4], rest[5:])
     bubbles = bubbles.reshape(states, slots, lanes).transpose(1, 0, 2)
     return fluid.reshape(comps, length, width, cells), bubbles, void.reshape(length, width, cells)
 

time: 70.5 us -> 66.1 us (0.938)
  the two profiles are of different devices: /device:TPU:14 before, /device:TPU:0 now
where the time goes in v2:
time: 66.1 us; the launch traced here: 65.5 us
  Pallas kernels  64.2 us (97%)
  between operations  1.28 us (2%)
    pallas_call x1, Pallas kernels, first_step(): pl.pallas_call(functools.partial(first_kernel, streams, azims, cap, lengt...  47.9 us
    pallas_call x1, Pallas kernels, second_step(): pl.pallas_call(functools.partial(second_kernel, devices, length), out_sha...  16.4 us

profile of v2, /device:TPU:0, one launch (start us, length us, event | category | flops | bytes accessed | tf_op | source)
XLA Modules:
  0.0 65.5 jit_solution(6414576615814558782)
XLA Ops:
  1.3 47.9 %first_step.1 = (f32[4,2048,128]{2,1,0:T(8,128)}, f32[2,2048,128]{2,1,0:T(8,128)}, f32[32,5,16,128]{3,2,1,0:T(8,128)}, f32[4,32,128]{2,1,0:T(8,128)}, f32[4,32,1...) custom-call(s32[512]{0:T(512)} %order_ref.1, ...), custom_call_target="tpu_custom_call" | custom-call | flops 16777216000 | bytes 12582912 | tf_op jit(solution)/shard_map/first_step/pallas_call | solution.py:751
  49.1 16.4 %second_step.1 = (f32[4,2048,128]{2,1,0:T(8,128)}, f32[2560,128]{1,0:T(8,128)}, f32[2048,128]{1,0:T(8,128)}) custom-call(s32[512]{0:T(512)} %tiles_ref.3, f32[2560,128]{1,0:T(8,128)} %bitcast.15, f32[2,2048,128]{2,1,0:T(8,128)} %get-tuple-element.18.rows_hbm, f32[4,2048,128]{2,1,0:T(8,128)} %get-tuple-element.19.flow_hbm, ...), custom_call_target="tpu_custom_call" | custom-call | flops 16777216000 | bytes 6291456 | tf_op jit(solution)/shard_map/second_step/pallas_call | solution.py:968

commit v3 on v2

--- a/solution.py
+++ b/solution.py
@@ -215,7 +215,7 @@
 def scatter(tile_rows, parts, tiles, store):
     cells_n = parts[0].shape[1]
     ids = lanes_of(tile_rows[...])
-    block = min(256, tiles)
+    block = min(1024, tiles)
     rhs = jnp.concatenate([x for part in parts for x in split_bf16(part[...])], axis=1)
 
     def some(i, carry):
@@ -847,10 +847,18 @@
     tile_v[:ahead, :] = jnp.full((ahead, lanes), -1.0, f32)
     rows_v[:ahead, :] = jnp.zeros((ahead, cells_n), f32)
     voids_v[:ahead, :] = jnp.zeros((ahead, cells_n), f32)
-    for load in (loads[1], *loads[7:]):
+    def store(n, src, dst):
+        copy = pltpu.make_async_copy(src, dst, store_sems.at[n])
+        copy.start()
+        return copy
+
+    for load in loads[1:]:
         load.wait()
+    add_halos(flow_v, 0, length, width, low_v, high_v, left_v, right_v)
     for copy in lists:
         copy.wait()
+    rest = pl.ds(1, comps - 1)
+    stores = [store(0, flow_v.at[rest], fluid_out.at[rest])]
     number = slots_ref[0, slots]
     chunks = (number + CHUNK - 1) // CHUNK
 
@@ -873,10 +881,15 @@
                 rows.append((rows_in[0, pl.ds(tile, 1), :], rows_in[1, pl.ds(tile, 1), :]))
             sample_quad(q, at, positions, columns, lambda j: rows[j], lhs, sp, su, sn)
 
-    def advance_start(i):
-        for _, at in groups(i):
-            state = [now_v[c, at, :] for c in range(STATES)]
-            drive, velocity = drive_of(sp[at, :], su[at, :], sn[at, :])
+    def ready(i):
+        return [
+            ([now_v[c, at, :] for c in range(STATES)], (sp[at, :], su[at, :], sn[at, :]))
+            for _, at in groups(i)
+        ]
+
+    def advance_start(i, loaded=None):
+        for (_, at), (state, sums) in zip(groups(i), loaded or ready(i)):
+            drive, velocity = drive_of(*sums)
             place, speed = travel(state[2], state[3], velocity)
             radius, growth = advance_group(state[0], state[1], state[4], drive, SUBSTEPS // 2)
             for c, x in enumerate((radius, growth, place, speed, state[4], drive)):
@@ -923,10 +936,11 @@
         sample(at_most(2))
 
         def steady(i, carry):
+            loaded = ready(i - 1)
+            sample(i)
             spread(i - 3)
             advance_end(i - 2)
-            advance_start(i - 1)
-            sample(i)
+            advance_start(i - 1, loaded)
             return carry
 
         lax.fori_loop(3, chunks, steady, 0)
@@ -937,16 +951,7 @@
         advance_end(before_end(1))
         spread(before_end(1))
 
-    def store(n, src, dst):
-        copy = pltpu.make_async_copy(src, dst, store_sems.at[n])
-        copy.start()
-        return copy
-
-    for load in loads[2:7]:
-        load.wait()
-    add_halos(flow_v, 0, length, width, low_v, high_v, left_v, right_v)
-    rest = pl.ds(1, comps - 1)
-    stores = [store(0, bubbles_v, bubbles_out), store(1, flow_v.at[rest], fluid_out.at[rest])]
+    stores.append(store(1, bubbles_v, bubbles_out))
 
     def finish(at, block, parts):
         rows = pl.ds(at, block)

time: 66.1 us -> 65.5 us (level)
  no operation moved by 1% of the time
where the time goes in v3:
time: 65.5 us; the launch traced here: 65.4 us
  Pallas kernels  64.2 us (98%)
  between operations  1.28 us (2%)
    pallas_call x1, Pallas kernels, first_step(): pl.pallas_call(functools.partial(first_kernel, streams, azims, cap, lengt...  47.8 us
    pallas_call x1, Pallas kernels, second_step(): pl.pallas_call(functools.partial(second_kernel, devices, length), out_sha...  16.4 us

profile of v3, /device:TPU:0, one launch (start us, length us, event | category | flops | bytes accessed | tf_op | source)
XLA Modules:
  0.0 65.4 jit_solution(4563467334958584596)
XLA Ops:
  1.3 47.8 %first_step.1 = (f32[4,2048,128]{2,1,0:T(8,128)}, f32[2,2048,128]{2,1,0:T(8,128)}, f32[32,5,16,128]{3,2,1,0:T(8,128)}, f32[4,32,128]{2,1,0:T(8,128)}, f32[4,32,1...) custom-call(s32[512]{0:T(512)} %order_ref.1, ...), custom_call_target="tpu_custom_call" | custom-call | flops 16777216000 | bytes 12582912 | tf_op jit(solution)/shard_map/first_step/pallas_call | solution.py:751
  49.0 16.4 %second_step.1 = (f32[4,2048,128]{2,1,0:T(8,128)}, f32[2560,128]{1,0:T(8,128)}, f32[2048,128]{1,0:T(8,128)}) custom-call(s32[512]{0:T(512)} %tiles_ref.3, f32[2560,128]{1,0:T(8,128)} %bitcast.15, f32[2,2048,128]{2,1,0:T(8,128)} %get-tuple-element.18.rows_hbm, f32[4,2048,128]{2,1,0:T(8,128)} %get-tuple-element.19.flow_hbm, ...), custom_call_target="tpu_custom_call" | custom-call | flops 16777216000 | bytes 6291456 | tf_op jit(solution)/shard_map/second_step/pallas_call | solution.py:973

commit v4 on v3

--- a/solution.py
+++ b/solution.py
@@ -744,7 +744,7 @@
     comps, tiles, cells = fluid.shape
     slots, lanes = order.shape[0], bubbles.shape[1]
     cap = slots // devices
-    soon = 3 * devices // 8
+    soon = 5 * devices // 16
     end, side = buffer(comps, width, cells), buffer(comps, length, cells)
     padded = buffer(comps, tiles + 2 * width, cells)
     per_slot = buffer(slots, lanes)

time: 65.5 us -> 65.7 us (level)
    pallas_call x1, Pallas kernels: 16.4 us -> 17.7 us  [second_step(): pl.pallas_call(functools.partial(second_kernel, devices, length), out_sha...]
    pallas_call x1, Pallas kernels: 47.8 us -> 46.5 us  [first_step(): pl.pallas_call(functools.partial(first_kernel, streams, azims, cap, lengt...]
where the time goes in v4:
time: 65.7 us; the launch traced here: 65.5 us
  Pallas kernels  64.2 us (98%)
  between operations  1.28 us (2%)
    pallas_call x1, Pallas kernels, first_step(): pl.pallas_call(functools.partial(first_kernel, streams, azims, cap, lengt...  46.5 us
    pallas_call x1, Pallas kernels, second_step(): pl.pallas_call(functools.partial(second_kernel, devices, length), out_sha...  17.7 us

profile of v4, /device:TPU:0, one launch (start us, length us, event | category | flops | bytes accessed | tf_op | source)
XLA Modules:
  0.0 65.5 jit_solution(7394969809095491909)
XLA Ops:
  1.3 46.5 %first_step.1 = (f32[4,2048,128]{2,1,0:T(8,128)}, f32[2,2048,128]{2,1,0:T(8,128)}, f32[32,5,16,128]{3,2,1,0:T(8,128)}, f32[4,32,128]{2,1,0:T(8,128)}, f32[4,32,1...) custom-call(s32[512]{0:T(512)} %order_ref.1, ...), custom_call_target="tpu_custom_call" | custom-call | flops 16777216000 | bytes 12582912 | tf_op jit(solution)/shard_map/first_step/pallas_call | solution.py:751
  47.8 17.7 %second_step.1 = (f32[4,2048,128]{2,1,0:T(8,128)}, f32[2560,128]{1,0:T(8,128)}, f32[2048,128]{1,0:T(8,128)}) custom-call(s32[512]{0:T(512)} %tiles_ref.3, f32[2560,128]{1,0:T(8,128)} %bitcast.15, f32[2,2048,128]{2,1,0:T(8,128)} %get-tuple-element.18.rows_hbm, f32[4,2048,128]{2,1,0:T(8,128)} %get-tuple-element.19.flow_hbm, ...), custom_call_target="tpu_custom_call" | custom-call | flops 16777216000 | bytes 6291456 | tf_op jit(solution)/shard_map/second_step/pallas_call | solution.py:973
